TPU v7x, 256 devices: a whole 4x4x8 slice. The times are simulated.
256 devices in a mesh: ctx: 32 (over z_lo, y, core), cp: 8 (over z_hi, x).
Axes of the slice: x: 4, y: 4, z: 8 (z_hi: 2, z_lo: 4; z = z_hi * 4 + z_lo), core: 2. Of those that a mesh axis runs over, the one named last changes fastest.
Arguments:
- signal: bfloat16 [524288, 128], P(('ctx', 'cp')), may hold values from -6 to 6
- gate: bfloat16 [524288, 128], P(('ctx', 'cp')), may hold values from -6 to 6
- filters: bfloat16 [2, 4096, 256, 128], P(None, ('ctx', 'cp')), as said below
- skip: float32 [128], replicated, may hold values from 0.5 to 1.5
Outputs:
- mixed: bfloat16 [524288, 128], P(('ctx', 'cp'))
Inputs may be any that keep to these rules, and one draw needn't show every extreme that they name: The filter spectra are those of real filters: response[(1048576 - k) % 1048576, c] is the complex conjugate of response[k, c] for every k and c.
All inputs are finite; a program needn't handle non-finite values.
Results may differ from a plain program's by a relative error of at most 0.001.
Values may be sent and summed in bfloat16 or wider, within the bound.
A program may use at most 128 MiB of HBM per device.

v0:
```python
import math

import jax
import jax.numpy as jnp
from jax import lax
from jax.sharding import PartitionSpec as P

HIGHEST = lax.Precision.HIGHEST


def twiddle_table(first, second, length, sign):
    product = first[:, None] * second[None, :] % length
    angle = sign * 2.0 * math.pi / length * product.astype(jnp.float32)
    return (jnp.cos(angle), jnp.sin(angle))


def twiddle_row(index, count, length, sign):
    product = index * jnp.arange(count, dtype=jnp.int32) % length
    angle = sign * 2.0 * math.pi / length * product.astype(jnp.float32)
    return (jnp.cos(angle), jnp.sin(angle))


def complex_apply(form, mat_re, mat_im, val_re, val_im):
    real = jnp.einsum(form, mat_re, val_re, precision=HIGHEST) - jnp.einsum(
        form, mat_im, val_im, precision=HIGHEST
    )
    imag = jnp.einsum(form, mat_re, val_im, precision=HIGHEST) + jnp.einsum(
        form, mat_im, val_re, precision=HIGHEST
    )
    return (real, imag)


def rotate(val_re, val_im, tab_re, tab_im):
    return (val_re * tab_re - val_im * tab_im, val_re * tab_im + val_im * tab_re)


def split_length(length):
    bits = length.bit_length() - 1
    first = 2 ** (bits // 2)
    return (first, length // first)


def forward_rows(real_rows, cols):
    first, second = split_length(cols)
    half = second // 2
    channels = real_rows.shape[1]
    blocks = real_rows.reshape(half, first, channels)
    fb_re, fb_im = twiddle_table(
        jnp.arange(second, dtype=jnp.int32), jnp.arange(half, dtype=jnp.int32), second, -1.0
    )
    z_re = jnp.einsum("kb,bac->kac", fb_re, blocks, precision=HIGHEST)
    z_im = jnp.einsum("kb,bac->kac", fb_im, blocks, precision=HIGHEST)
    tw_re, tw_im = twiddle_table(
        jnp.arange(second, dtype=jnp.int32), jnp.arange(first, dtype=jnp.int32), cols, -1.0
    )
    z_re, z_im = rotate(z_re, z_im, tw_re[:, :, None], tw_im[:, :, None])
    fa_re, fa_im = twiddle_table(
        jnp.arange(first, dtype=jnp.int32), jnp.arange(first, dtype=jnp.int32), first, -1.0
    )
    out_re, out_im = complex_apply("ya,kac->ykc", fa_re, fa_im, z_re, z_im)
    return (out_re.reshape(cols, channels), out_im.reshape(cols, channels))


def inverse_rows(val_re, val_im, full):
    cols, channels = val_re.shape
    first, second = split_length(cols)
    half = second // 2
    grid_re = val_re.reshape(first, second, channels)
    grid_im = val_im.reshape(first, second, channels)
    fa_re, fa_im = twiddle_table(
        jnp.arange(first, dtype=jnp.int32), jnp.arange(first, dtype=jnp.int32), first, 1.0
    )
    z_re, z_im = complex_apply("ay,ykc->akc", fa_re, fa_im, grid_re, grid_im)
    tw_re, tw_im = twiddle_table(
        jnp.arange(first, dtype=jnp.int32), jnp.arange(second, dtype=jnp.int32), cols, 1.0
    )
    z_re, z_im = rotate(z_re, z_im, tw_re[:, :, None], tw_im[:, :, None])
    fb_re, fb_im = twiddle_table(
        jnp.arange(half, dtype=jnp.int32), jnp.arange(second, dtype=jnp.int32), second, 1.0
    )
    rows = jnp.einsum("bk,akc->bac", fb_re, z_re, precision=HIGHEST) - jnp.einsum(
        "bk,akc->bac", fb_im, z_im, precision=HIGHEST
    )
    rows = rows.reshape(half * first, channels) * (1.0 / full)
    other = jnp.einsum("bk,akc->bac", fb_re, z_im, precision=HIGHEST) + jnp.einsum(
        "bk,akc->bac", fb_im, z_re, precision=HIGHEST
    )
    return (rows, other.reshape(half * first, channels) * (1.0 / full))


def fold_mirror(values, blocks):
    cols = values.shape[0]
    rest = values.shape[1:]
    half = cols // 2
    piece = cols // blocks // 2
    lower = values[:half].reshape((blocks, piece) + rest)
    upper = jnp.concatenate([values[half : half + 1], values[half + 1 :][::-1]], axis=0)
    upper = upper.reshape((blocks, piece) + rest)
    return jnp.stack([lower, upper], axis=1).reshape(values.shape)


def unfold_mirror(values, blocks):
    cols = values.shape[0]
    rest = values.shape[1:]
    half = cols // 2
    piece = cols // blocks // 2
    both = values.reshape((blocks, 2, piece) + rest)
    lower = both[:, 0].reshape((half,) + rest)
    upper = both[:, 1].reshape((half,) + rest)
    return jnp.concatenate([lower, upper[:1], upper[1:][::-1]], axis=0)


def reflect_locally(values, position_slot):
    width = values.shape[0]
    piece = width // 2
    generic = jnp.concatenate([values[piece:], values[:piece]], axis=0)[:, ::-1]
    first = jnp.roll(values[0][::-1], 1, axis=0)
    nyquist_row = values[piece][::-1]
    fixed = generic.at[0].set(first).at[piece].set(nyquist_row)
    return jnp.where(position_slot == 0, fixed, generic)


def body(signal, gate, filters, skip):
    ctx_count = lax.axis_size("ctx")
    cp_count = lax.axis_size("cp")
    devices = ctx_count * cp_count
    position_slot = lax.axis_index("ctx") * cp_count + lax.axis_index("cp")
    seq_rows, channels = signal.shape
    reps = seq_rows // devices
    cols = 2 * seq_rows
    full = cols * devices
    width = cols // devices
    paired = channels // 2
    local = signal.reshape(reps, devices, channels)
    moved = lax.all_to_all(
        lax.all_to_all(local, "ctx", split_axis=1, concat_axis=0, tiled=True),
        "cp",
        split_axis=1,
        concat_axis=0,
        tiled=True,
    )
    rows = (
        moved.reshape(cp_count, ctx_count, reps, channels)
        .transpose(1, 0, 2, 3)
        .reshape(seq_rows, channels)
    )
    spec_re, spec_im = forward_rows(rows.astype(jnp.float32), cols)
    spec_re, spec_im = (
        spec_re[:, :paired] - spec_im[:, paired:],
        spec_im[:, :paired] + spec_re[:, paired:],
    )
    row_re, row_im = twiddle_row(position_slot, cols, full, -1.0)
    spec_re, spec_im = rotate(spec_re, spec_im, row_re[:, None], row_im[:, None])
    spec_re = fold_mirror(spec_re, devices)
    spec_im = fold_mirror(spec_im, devices)
    stacked = jnp.stack([spec_re, spec_im])[:, :, None, :]
    got = lax.all_to_all(
        lax.all_to_all(stacked, "ctx", split_axis=1, concat_axis=2, tiled=True),
        "cp",
        split_axis=1,
        concat_axis=2,
        tiled=True,
    )
    slots = jnp.arange(devices, dtype=jnp.int32)
    source = slots % ctx_count * cp_count + slots // ctx_count
    fk_re, fk_im = twiddle_table(jnp.arange(devices, dtype=jnp.int32), source, devices, -1.0)
    spectral_real, spectral_imaginary = complex_apply("kj,sjc->skc", fk_re, fk_im, got[0], got[1])
    filt_re = filters[0].astype(jnp.float32)
    filt_im = filters[1].astype(jnp.float32)
    reflected_real = reflect_locally(spectral_real, position_slot)
    reflected_imaginary = -reflect_locally(spectral_imaginary, position_slot)
    leading_real = 0.5 * (spectral_real + reflected_real)
    leading_imaginary = 0.5 * (spectral_imaginary + reflected_imaginary)
    partner_real = 0.5 * (spectral_imaginary - reflected_imaginary)
    partner_imaginary = -0.5 * (spectral_real - reflected_real)
    lead_re = leading_real * filt_re[..., :paired] - leading_imaginary * filt_im[..., :paired]
    lead_im = leading_real * filt_im[..., :paired] + leading_imaginary * filt_re[..., :paired]
    tail_re = partner_real * filt_re[..., paired:] - partner_imaginary * filt_im[..., paired:]
    tail_im = partner_real * filt_im[..., paired:] + partner_imaginary * filt_re[..., paired:]
    prod_re = lead_re - tail_im
    prod_im = lead_im + tail_re
    lanes = prod_re.shape[-1]
    fi_re, fi_im = twiddle_table(
        jnp.arange(devices, dtype=jnp.int32), jnp.arange(devices, dtype=jnp.int32), devices, 1.0
    )
    back_re, back_im = complex_apply("rk,skc->src", fi_re, fi_im, prod_re, prod_im)
    returned = lax.all_to_all(
        lax.all_to_all(
            jnp.stack([back_re, back_im]), "ctx", split_axis=2, concat_axis=1, tiled=True
        ),
        "cp",
        split_axis=2,
        concat_axis=1,
        tiled=True,
    )
    returned = (
        returned.reshape(2, cp_count, ctx_count, width, lanes)
        .transpose(0, 2, 1, 3, 4)
        .reshape(2, cols, lanes)
    )
    ret_re = unfold_mirror(returned[0], devices)
    ret_im = unfold_mirror(returned[1], devices)
    back_tw_re, back_tw_im = twiddle_row(position_slot, cols, full, 1.0)
    ret_re, ret_im = rotate(ret_re, ret_im, back_tw_re[:, None], back_tw_im[:, None])
    conv_re, conv_im = inverse_rows(ret_re, ret_im, full)
    conv = jnp.concatenate([conv_re, conv_im], axis=1)
    arrived = lax.all_to_all(
        lax.all_to_all(conv[:, None, :], "ctx", split_axis=0, concat_axis=1, tiled=True),
        "cp",
        split_axis=0,
        concat_axis=1,
        tiled=True,
    )
    conv_local = (
        arrived.reshape(reps, cp_count, ctx_count, channels)
        .transpose(0, 2, 1, 3)
        .reshape(seq_rows, channels)
    )
    mixed = gate.astype(jnp.float32) * (conv_local + skip[None, :] * signal.astype(jnp.float32))
    return mixed.astype(jnp.bfloat16)


def solution(mesh):
    placed = (
        P(("ctx", "cp"), None),
        P(("ctx", "cp"), None),
        P(None, ("ctx", "cp"), None, None),
        P(),
    )
    return jax.shard_map(
        body, mesh=mesh, in_specs=placed, out_specs=P(("ctx", "cp"), None), check_vma=False
    )
```

profile of v0, /device:TPU:32, one launch (start us, length us, event | category | flops | bytes accessed | tf_op | source)
XLA Modules:
  0.0 582.3 jit_solution(10288295839334694450)
XLA Ops:
  1.4 23.9 %all_to_all.129 = bf16[8,256,128]{2,0,1:T(8,128)(2,1)S(1)} all-to-all(bf16[8,256,128]{2,0,1:T(8,128)(2,1)S(1)} %copy.175), channel_id=1, replica_groups=mesh['ctx'=32,'cp'=8] {'ctx'}, dimensions={1} | all-to-all | bytes 1048576 | tf_op jit(solution)/shard_map/all_to_all | solution.py:136
  26.3 8.2 %all-to-all-start.1 = ((bf16[256,8,128]{2,0,1:T(8,128)(2,1)}), bf16[256,8,128]{2,0,1:T(8,128)(2,1)S(1)}, u32[]{:S(2)}, u32[]{:S(2)}) async-start(bf16[256,8,128]{2,0,1:T(8,128)(2,1)} %copy.178), calls=%async_computation.1 | async-start | bytes 1048576 | tf_op jit(solution)/shard_map/all_to_all | solution.py:135
  35.1 18.9 %all-to-all-done.1 = bf16[256,8,128]{2,0,1:T(8,128)(2,1)S(1)} async-done(((bf16[256,8,128]{2,0,1:T(8,128)(2,1)}), bf16[256,8,128]{2,0,1:T(8,128)(2,1)S(1)}, u32[]{:S(2)}, u32[]{:S(2)}) %all-to-all-start.1) | async-done | bytes 524320 | tf_op jit(solution)/shard_map/all_to_all | solution.py:135
  82.5 16.1 %copy.278 = f32[2,4096,1,64]{3,0,2,1:T(2,128)} copy(f32[2,4096,1,64]{3,1,0,2:T(8,128)S(1)} %maximum_bitcast_fusion) | data formatting | bytes 4194304 | tf_op jit(solution)/shard_map/broadcast_in_dim | solution.py:156
  98.6 5.8 reshape.329
  104.4 51.6 %all_to_all.130 = f32[32,1,16384]{2,1,0:T(1,128)} all-to-all(f32[32,1,16384]{2,1,0:T(1,128)S(1)} %reshape.329), channel_id=1, replica_groups=mesh['ctx'=32,'cp'=8] {'ctx'}, dimensions={0} | all-to-all | bytes 4194304 | tf_op jit(solution)/shard_map/all_to_all | solution.py:158
  156.6 7.4 %reduce.8 = f32[32,16384]{1,0:T(8,128)S(1)} reduce(f32[32,1,16384]{2,1,0:T(1,128)} %all_to_all.130, f32[]{:T(128)} %broadcast.483), dimensions={1}, to_apply=%all_to_all.101.reduce_sub_computation | reduce | bytes 4194308 | tf_op jit(solution)/shard_map/all_to_all | solution.py:158
  164.0 4.5 reshape.330
  168.4 6.6 %copy.277 = f32[2,32,128,1,64]{4,1,0,2,3:T(8,128)} copy(f32[2,32,128,1,64]{4,0,2,1,3:T(2,128)} %bitcast.233) | data formatting | bytes 4194304 | tf_op jit(solution)/shard_map/all_to_all | solution.py:158
  175.0 7.2 %reshape.331 = f32[8,1,65536]{2,1,0:T(1,128)} reshape(f32[128,2,32,64]{3,2,1,0:T(8,128)} %bitcast.234) | data formatting | bytes 4194304
  182.2 4.4 all-to-all-start.3
  192.2 46.4 %all-to-all-done.3 = f32[8,1,65536]{2,1,0:T(1,128)} async-done(((f32[8,1,65536]{2,1,0:T(1,128)}), f32[8,1,65536]{2,1,0:T(1,128)}, u32[]{:S(2)}, u32[]{:S(2)}) %all-to-all-start.3) | async-done | bytes 2097184 | tf_op jit(solution)/shard_map/all_to_all | solution.py:157
  238.6 7.2 %reduce.9 = f32[8,65536]{1,0:T(8,128)S(1)} reduce(f32[8,1,65536]{2,1,0:T(1,128)} %all-to-all-done.3, f32[]{:T(128)} %broadcast.483), dimensions={1}, to_apply=%all_to_all.105.reduce_sub_computation | reduce | bytes 4194308 | tf_op jit(solution)/shard_map/all_to_all | solution.py:157
  245.8 3.7 reshape.332
  253.2 4.4 fusion.56
  257.6 4.3 fusion.37
  262.7 4.2 fusion.54
  266.9 4.3 fusion.36
  286.5 4.0 add_subtract_fusion
  298.6 4.5 copy.205
  303.0 4.9 reshape.333
  307.9 52.8 %all_to_all.131 = f32[32,1,16384]{2,1,0:T(1,128)} all-to-all(f32[32,1,16384]{2,1,0:T(1,128)S(1)} %reshape.333), channel_id=1, replica_groups=mesh['ctx'=32,'cp'=8] {'ctx'}, dimensions={0} | all-to-all | bytes 4194304 | tf_op jit(solution)/shard_map/all_to_all | solution.py:188
  360.7 7.4 %reduce.10 = f32[32,16384]{1,0:T(8,128)S(1)} reduce(f32[32,1,16384]{2,1,0:T(1,128)} %all_to_all.131, f32[]{:T(128)} %broadcast.483), dimensions={1}, to_apply=%all_to_all.108.reduce_sub_computation | reduce | bytes 4194308 | tf_op jit(solution)/shard_map/all_to_all | solution.py:188
  371.2 6.6 %copy.207 = f32[2,32,16,8,64]{4,3,2,1,0:T(8,128)} copy(f32[2,32,16,8,64]{4,2,0,3,1:T(8,128)} %bitcast.236) | data formatting | bytes 4194304 | tf_op jit(solution)/shard_map/all_to_all | solution.py:188
  377.7 3.8 copy.208
  381.5 6.0 %all-to-all-start.5 = ((f32[2,512,8,64]{1,3,0,2:T(8,128)}), f32[2,512,8,64]{1,3,0,2:T(8,128)S(1)}, u32[]{:S(2)}, u32[]{:S(2)}) async-start(f32[2,512,8,64]{1,3,0,2:T(8,128)} %copy.208), calls=%async_computation.5 | async-start | bytes 4194304 | tf_op jit(solution)/shard_map/all_to_all | solution.py:187
  388.1 51.9 %all-to-all-done.5 = f32[2,512,8,64]{1,3,0,2:T(8,128)S(1)} async-done(((f32[2,512,8,64]{1,3,0,2:T(8,128)}), f32[2,512,8,64]{1,3,0,2:T(8,128)S(1)}, u32[]{:S(2)}, u32[]{:S(2)}) %all-to-all-start.5) | async-done | bytes 2097184 | tf_op jit(solution)/shard_map/all_to_all | solution.py:187
  454.3 8.7 %reverse.6 = f32[2048,64]{0,1:T(8,128)} reverse(f32[2048,64]{0,1:T(8,128)} %bitcast.247), dimensions={0} | reverse | bytes 1048576
  469.8 4.3 multiply_subtract_fusion.1
  496.8 3.6 fusion.25
  512.7 29.4 %all_to_all.132 = f32[2048,1,128]{2,1,0:T(1,128)S(1)} all-to-all(f32[2048,1,128]{2,1,0:T(1,128)S(1)} %copy.230), channel_id=1, replica_groups=mesh['ctx'=32,'cp'=8] {'ctx'}, dimensions={0} | all-to-all | bytes 2097152 | tf_op jit(solution)/shard_map/all_to_all | solution.py:208
  542.7 37.5 %all_to_all.133 = f32[64,32,128]{2,1,0:T(8,128)S(1)} all-to-all(f32[64,32,128]{2,1,0:T(8,128)S(1)} %copy.231), channel_id=1, replica_groups=mesh['ctx'=32,'cp'=8] {'cp'}, dimensions={0} | all-to-all | bytes 2097152 | tf_op jit(solution)/shard_map/all_to_all | solution.py:207
  (140 shorter events, 126.8 us)
Async XLA Ops:
  26.3 27.7 %all-to-all-start.1 = ((bf16[256,8,128]{2,0,1:T(8,128)(2,1)}), bf16[256,8,128]{2,0,1:T(8,128)(2,1)S(1)}, u32[]{:S(2)}, u32[]{:S(2)}) async-start(bf16[256,8,128]{2,0,1:T(8,128)(2,1)} %copy.178), calls=%async_computation.1 | async-start | bytes 1048576 | tf_op jit(solution)/shard_map/all_to_all | solution.py:135
  79.5 1.2 copy-start.7
  80.8 1.2 copy-start.6
  182.2 56.4 %all-to-all-start.3 = ((f32[8,1,65536]{2,1,0:T(1,128)}), f32[8,1,65536]{2,1,0:T(1,128)}, u32[]{:S(2)}, u32[]{:S(2)}) async-start(f32[8,1,65536]{2,1,0:T(1,128)} %reshape.331), calls=%async_computation.3 | async-start | bytes 4194304 | tf_op jit(solution)/shard_map/all_to_all | solution.py:157
  275.5 2.9 copy-start.2
  280.7 2.8 copy-start.3
  381.5 58.5 %all-to-all-start.5 = ((f32[2,512,8,64]{1,3,0,2:T(8,128)}), f32[2,512,8,64]{1,3,0,2:T(8,128)S(1)}, u32[]{:S(2)}, u32[]{:S(2)}) async-start(f32[2,512,8,64]{1,3,0,2:T(8,128)} %copy.208), calls=%async_computation.5 | async-start | bytes 4194304 | tf_op jit(solution)/shard_map/all_to_all | solution.py:187
  451.8 13.2 %copy-start.5 = (f32[2048,64]{1,0:T(8,128)S(1)}, f32[2048,64]{1,0:T(8,128)}, u32[]{:S(2)}) copy-start(f32[2048,64]{1,0:T(8,128)} %get-tuple-element.70) | copy-start | bytes 1572868
  477.4 3.4 copy-start
  484.4 2.1 copy-start.4
  486.5 2.2 copy-start.1
  509.2 2.7 copy-start.8
  542.7 38.1 %copy-start.9 = (bf16[2048,128]{1,0:T(8,128)(2,1)S(1)}, bf16[2048,128]{1,0:T(8,128)(2,1)}, u32[]{:S(2)}) copy-start(bf16[2048,128]{1,0:T(8,128)(2,1)} %param.12) | copy-start | bytes 1572868
  542.7 38.1 %copy-start.10 = (bf16[2048,128]{1,0:T(8,128)(2,1)S(1)}, bf16[2048,128]{1,0:T(8,128)(2,1)}, u32[]{:S(2)}) copy-start(bf16[2048,128]{1,0:T(8,128)(2,1)} %param.13) | copy-start | bytes 1572868
  542.7 38.1 %copy-start.11 = (f32[128]{0:T(128)S(1)}, f32[128]{0:T(128)}, u32[]{:S(2)}) copy-start(f32[128]{0:T(128)} %param.15) | copy-start | bytes 1540
where the time goes:
time: 594 us; the launch traced here: 582 us
  blocking collectives  195 us (33%)
  local copies, waits for them, and re-layouts  143 us (24%)
  waiting for transfers between devices  117 us (20%)
  matrix products  63.8 us (11%)
  other arithmetic  43.7 us (7%)
  starting transfers between devices  18.6 us (3%)
    all_to_all x1, blocking collectives, body(): lax.all_to_all(jnp.stack([back_re, back_im]), 'ctx', split_axis=2, concat...  52.8 us
    all_to_all x1, waiting for transfers between devices, body(): lax.all_to_all(lax.all_to_all(jnp.stack([back_re, back_im]), 'ctx', split...  51.9 us
    all_to_all x1, blocking collectives, body(): lax.all_to_all(stacked, 'ctx', split_axis=1, concat_axis=2, tiled=True)  51.6 us
    unnamed x45, local copies, waits for them, and re-layouts  50.9 us
    all_to_all x1, waiting for transfers between devices, body(): lax.all_to_all(lax.all_to_all(stacked, 'ctx', split_axis=1, concat_axis=2...  46.4 us
    all_to_all x1, blocking collectives, body(): lax.all_to_all(lax.all_to_all(conv[:, None, :], 'ctx', split_axis=0, conc...  37.5 us
    all_to_all x1, blocking collectives, body(): lax.all_to_all(conv[:, None, :], 'ctx', split_axis=0, concat_axis=1, tile...  29.4 us
    all_to_all x1, blocking collectives, body(): lax.all_to_all(local, 'ctx', split_axis=1, concat_axis=0, tiled=True)  23.9 us
  transfers between devices with their start and end apart: 3, of which 3 were waited for; matrix products, arithmetic and copies ran while one was open for 1% of the time, Pallas kernels for 0%

commit v1 on v0

v1 whole, which is shorter than its diff:
```python
import functools
import math

import jax
import jax.numpy as jnp
import ml_dtypes
import numpy as np
from jax import lax
from jax.experimental import pallas as pl
from jax.experimental.pallas import tpu as pltpu
from jax.sharding import PartitionSpec as P


FULL = 1 << 20
ROWS = 144
F32 = jnp.float32
BF16 = jnp.bfloat16

LOW = ((2, 4, 6, 0), (3, 5, 7, 1))
UPP = ((6, 4, 2, 0), (5, 3, 1, 7))


def phase(product, length):
    angle = 2 * math.pi * (np.asarray(product, dtype=np.int64) % length) / length
    return np.cos(angle), np.sin(angle)


def split_np(array):
    high = array.astype(ml_dtypes.bfloat16)
    low = (array - high.astype(np.float64)).astype(ml_dtypes.bfloat16)
    return high, low


def row_sigma(core):
    index = np.concatenate([4 * np.arange(32) + t for t in (1, 2, 3, 0)] + [np.array([128])])
    sigma = 2 * index + core
    if core == 1:
        sigma[128] = 0
    return sigma


@functools.lru_cache(maxsize=None)
def tables():
    pos = np.arange(256)
    core_of, chip_of = pos // 128, pos % 128
    block = ((chip_of // 8) * 2 + core_of) * 8 + chip_of % 8
    m256 = []
    tb = np.zeros((2, 2, ROWS, 256), np.float32)
    ta = np.zeros((2, ROWS, 128), np.float32)
    beta, al = np.arange(256), np.arange(8)
    for core in (0, 1):
        sigma = row_sigma(core)
        cos, sin = phase(sigma[:128, None] * block[None, :], 512)
        fwd = np.concatenate([cos, -sin], 0)
        inv = np.concatenate([cos.T, -sin.T], 1)
        if core == 0:
            nyquist = phase(256 * block, 512)[0]
            fwd[128 + 96] = nyquist
            inv[:, 128 + 96] = nyquist
        inv = inv * (2.0 / FULL)
        m256.append(np.stack([*split_np(fwd), *split_np(inv)]))
        cos, sin = phase(sigma[:, None] * beta[None, :], FULL)
        tb[core, 0, :129], tb[core, 1, :129] = cos, -sin
        cos, sin = phase(sigma[:, None] * al[None, :], 4096)
        ta[core, :129, 0:8], ta[core, :129, 8:16] = cos, -sin
    cos, sin = phase(beta[:, None] * beta[None, :], 256)
    m512 = np.stack(
        [
            *split_np(np.block([[cos, -sin], [sin, cos]])),
            *split_np(np.block([[cos, sin], [-sin, cos]])),
        ]
    )
    cos, sin = phase(al[:, None] * beta[None, :], 2048)
    t2 = np.stack([cos, -sin]).astype(np.float32)
    return np.stack(m256), m512, tb, ta, t2


def cmul(a, b, c, d):
    return a * c - b * d, a * d + b * c


def dft8(re, im, sign):
    root = math.sqrt(0.5)

    def turn(x, y, power):
        if power == 0:
            return x, y
        if power == 2:
            return (-y, x) if sign > 0 else (y, -x)
        if power == 1:
            if sign > 0:
                return (x - y) * root, (x + y) * root
            return (x + y) * root, (y - x) * root
        if sign > 0:
            return (-x - y) * root, (x - y) * root
        return (y - x) * root, (-x - y) * root

    def step(res, ims):
        n = len(res)
        if n == 1:
            return res, ims
        h = n // 2
        er = [res[j] + res[j + h] for j in range(h)]
        ei = [ims[j] + ims[j + h] for j in range(h)]
        odd = [turn(res[j] - res[j + h], ims[j] - ims[j + h], j * (8 // n)) for j in range(h)]
        er, ei = step(er, ei)
        dr, di = step([o[0] for o in odd], [o[1] for o in odd])
        outr, outi = [], []
        for j in range(h):
            outr += [er[j], dr[j]]
            outi += [ei[j], di[j]]
        return outr, outi

    return step(re, im)


def split(x):
    high = x.astype(BF16)
    return high, (x - high.astype(F32)).astype(BF16)


def dot(a, b):
    return jnp.dot(a, b, preferred_element_type=F32)


def kernel(
    sig, filt, gate, skip, m256, m512, tb, ta, t2, out,
    fv, ev, gv, m256v, m512v, tbv, tav, t2v,
    s32, xs, xb, x32, fs, es, hb, eb, hf, fz, tw, zh, zl, gg, ce, ch, cl,
    yo, yw, ys, pb, yb, lsem, ssem, rsem,
):
    ctx, cp = lax.axis_index("ctx"), lax.axis_index("cp")
    core = lax.rem(ctx, 2)
    other = 1 - core
    chip = (ctx // 2) * 8 + cp
    here = ctx * 8 + cp
    even = (1 - core).astype(F32)

    def device(t, k):
        return ((t // 8) * 2 + k, lax.rem(t, 8))

    def remote(src, dst, sem, t, k):
        return pltpu.make_async_remote_copy(
            src_ref=src, dst_ref=dst, send_sem=ssem.at[sem], recv_sem=rsem.at[sem],
            device_id=device(t, k), device_id_type=pl.DeviceIdType.MESH,
        )

    def loop(n, body, start=0):
        def wrapped(i, carry):
            body(i)
            return carry

        lax.fori_loop(start, n, wrapped, 0)

    barrier = pltpu.get_barrier_semaphore()

    def greet(i):
        t = lax.rem(here + i, 256)
        pl.semaphore_signal(
            barrier, inc=1, device_id=(t // 8, lax.rem(t, 8)), device_id_type=pl.DeviceIdType.MESH
        )

    loop(256, greet, 1)

    group, place = here // 64, lax.rem(here, 64)
    upper = (place >= 32).astype(jnp.int32)
    loads = [
        pltpu.make_async_copy(filt.at[:, pl.ds(upper * 8, 8)], fv, lsem.at[0]),
        pltpu.make_async_copy(filt.at[:, pl.ds(8, 1)], ev, lsem.at[1]),
        pltpu.make_async_copy(ta.at[core], tav, lsem.at[2]),
        pltpu.make_async_copy(tb.at[core], tbv, lsem.at[3]),
        pltpu.make_async_copy(m256.at[core], m256v, lsem.at[4]),
        pltpu.make_async_copy(m512, m512v, lsem.at[5]),
        pltpu.make_async_copy(t2, t2v, lsem.at[6]),
        pltpu.make_async_copy(gate, gv, lsem.at[7]),
    ]
    for load in loads:
        load.start()

    def turn_signal(a):
        block = sig[pl.ds(pl.multiple_of(a * 128, 128), 128), :].astype(F32)
        s32[pl.ds(a, 128, stride=16), :] = block.T

    loop(16, turn_signal)

    def pack(dst, base):
        def body(i):
            rows = s32[pl.ds(pl.multiple_of(i * 256, 256), 256), :]
            dst[pl.ds(base + i * 16, 16)] = rows.astype(BF16).reshape(16, 16, 128)

        loop(8, body)

    pack(xs, 0)

    loads[0].wait()
    loads[1].wait()

    def turn_filter(k):
        for blk in range(4):
            row = jnp.where(upper == 1, UPP[k][blk], LOW[k][blk])

            def body(j, row=row, blk=blk):
                ri, qh = j // 2, lax.rem(j, 2)
                block = fv[ri, row, pl.ds(pl.multiple_of(qh * 128, 128), 128), :].astype(F32)
                s32[pl.ds(ri * 8 + blk * 2 + qh, 128, stride=16), :] = block.T

            loop(4, body)

    for k in range(2):
        turn_filter(k)
        pack(fs, k * 128)

    @pl.when(here == 0)
    def _():
        def body(j):
            ri, qh = j // 2, lax.rem(j, 2)
            block = ev[ri, 0, pl.ds(pl.multiple_of(qh * 128, 128), 128), :].astype(F32).T
            for blk in range(4):
                s32[pl.ds(ri * 8 + blk * 2 + qh, 128, stride=16), :] = block

        loop(4, body)
        pack(es, 0)

    loads[2].wait()
    loads[3].wait()

    def make_twiddle(r):
        rows = pl.ds(pl.multiple_of(r * 16, 16), 16)
        cols = tav[rows, :]
        for al in range(8):
            c = jnp.broadcast_to(cols[:, al : al + 1], (16, 256))
            s = jnp.broadcast_to(cols[:, 8 + al : 9 + al], (16, 256))
            tw[al, 0, rows, :], tw[al, 1, rows, :] = cmul(c, s, tbv[0, rows, :], tbv[1, rows, :])

    loop(9, make_twiddle)

    pl.semaphore_wait(barrier, 255)
    slot = core * 128 + chip

    def send_signal(i):
        t = lax.rem(chip + i, 128)
        remote(xs.at[t], xb.at[slot], 0, t, core).start()

    pltpu.make_async_copy(xs.at[chip], xb.at[slot], rsem.at[0]).start()
    loop(128, send_signal, 1)

    fslot = jnp.where(upper == 1, (7 - group) * 32 + 63 - place, group * 32 + place)

    def send_filter(i):
        t = lax.rem(chip + i, 128)
        for k in range(2):
            remote(fs.at[k * 128 + t], hb.at[fslot], 1, t, k).start()

    pltpu.make_async_copy(fs.at[core * 128 + chip], hb.at[fslot], rsem.at[1]).start()
    remote(fs.at[other * 128 + chip], hb.at[fslot], 1, chip, other).start()
    loop(128, send_filter, 1)

    @pl.when(here == 0)
    def _():
        def body(t):
            remote(es.at[t], eb.at[0], 2, t, 0).start()

        pltpu.make_async_copy(es.at[0], eb.at[0], rsem.at[2]).start()
        loop(128, body, 1)

    mine = xb.at[pl.ds(core * 128, 128)]
    theirs = xb.at[pl.ds(other * 128, 128)]
    pltpu.make_async_copy(mine, mine, rsem.at[0]).wait()
    forward = remote(mine, mine, 3, chip, other)
    forward.start()
    for load in loads[4:]:
        load.wait()
    pltpu.make_async_copy(theirs, theirs, rsem.at[3]).wait()

    def widen(src, dst):
        def body(i):
            dst[pl.ds(pl.multiple_of(i * 256, 256), 256), :] = (
                src[pl.ds(i * 16, 16)].astype(F32).reshape(256, 128)
            )

        loop(16, body)

    widen(xb, x32)

    top = (lax.broadcasted_iota(jnp.int32, (8, 256), 0) == 0).astype(F32)

    def first(al):
        x = jnp.concatenate(
            [x32[pl.ds(2 * al, 256, stride=16), :], x32[pl.ds(2 * al + 1, 256, stride=16), :]], 1
        ).astype(BF16)
        f = dot(m256v[0], x) + dot(m256v[1], x)
        fz[al, 0, 0:128, :] = f[0:128]
        fz[al, 1, 0:128, :] = f[128:256]
        lone = f[224:232] * (top * even)
        fz[al, 1, 96:104, :] = f[224:232] - lone
        fz[al, 0, 128:136, :] = lone
        fz[al, 0, 136:144, :] = jnp.zeros((8, 256), F32)
        fz[al, 1, 128:144, :] = jnp.zeros((16, 256), F32)

    loop(8, first)

    def second(r):
        rows = pl.ds(pl.multiple_of(r * 16, 16), 16)
        for half in range(2):
            ln = slice(half * 128, half * 128 + 128)
            lm = slice(256 + half * 128, 384 + half * 128)
            pairs = [
                cmul(fz[al, 0, rows, ln], fz[al, 1, rows, ln], tw[al, 0, rows, ln], tw[al, 1, rows, ln])
                for al in range(8)
            ]
            re, im = dft8([p[0] for p in pairs], [p[1] for p in pairs], -1)
            for e in range(8):
                a, b = re[e], im[e]
                if e:
                    a, b = cmul(a, b, t2v[0, e : e + 1, ln], t2v[1, e : e + 1, ln])
                zh[e, rows, ln], zl[e, rows, ln] = split(a)
                zh[e, rows, lm], zl[e, rows, lm] = split(b)

    loop(9, second)

    def third(base):
        def body(j):
            a = zh[pl.ds(j * 2, 2)].reshape(2 * ROWS, 512)
            b = zl[pl.ds(j * 2, 2)].reshape(2 * ROWS, 512)
            g = dot(a, m512v[base]) + dot(a, m512v[base + 1]) + dot(b, m512v[base])
            gg[pl.ds(j * 2, 2)] = g.reshape(2, ROWS, 512)

        loop(4, body)

    third(0)

    pltpu.make_async_copy(hb, hb, rsem.at[1]).wait()
    widen(hb, x32)

    def place_filter(e, shift):
        for ri in range(2):
            hf[e, ri, 128:144, :] = jnp.zeros((16, 256), F32)
            if shift:
                hf[e, ri, 96:104, :] = jnp.zeros((8, 256), F32)
            for blk in range(4):
                lo = blk * 32 + (1 if shift and blk == 3 else 0)
                for qh in range(2):
                    start = e * 512 + (ri * 8 + blk * 2 + qh)
                    hf[e, ri, lo : lo + 32, qh * 128 : qh * 128 + 128] = x32[
                        pl.ds(start, 32, stride=16), :
                    ]

    loop(4, lambda e: place_filter(e, False))

    @pl.when(core == 1)
    def _():
        loop(8, lambda e: place_filter(e, False), 4)

    @pl.when(core == 0)
    def _():
        loop(8, lambda e: place_filter(e, True), 4)
        pltpu.make_async_copy(eb, eb, rsem.at[2]).wait()
        extra = eb[0].astype(F32)
        for ri in range(2):
            hf[0, ri, 96:97, :] = hf[0, ri, 96:97, :] * 0.5
            for qh in range(2):
                row = ri * 8 + 6 + qh
                hf[4, ri, 96:97, qh * 128 : qh * 128 + 128] = extra[row : row + 1] * 0.5

    def apply_filter(e):
        def body(r):
            rows = pl.ds(pl.multiple_of(r * 16, 16), 16)
            a, b = cmul(
                gg[e, rows, 0:256], gg[e, rows, 256:512], hf[e, 0, rows, :], hf[e, 1, rows, :]
            )
            zh[e, rows, 0:256], zl[e, rows, 0:256] = split(a)
            zh[e, rows, 256:512], zl[e, rows, 256:512] = split(b)

        loop(9, body)

    loop(8, apply_filter)
    third(2)

    def back(r, last):
        rows = pl.ds(r * 16, 16) if last else pl.ds(pl.multiple_of(r * 16, 16), 16)
        for half in range(2):
            ln = slice(half * 128, half * 128 + 128)
            lm = slice(256 + half * 128, 384 + half * 128)
            re, im = [], []
            for e in range(8):
                a, b = gg[e, rows, ln], gg[e, rows, lm]
                if e:
                    a, b = cmul(a, b, t2v[0, e : e + 1, ln], -t2v[1, e : e + 1, ln])
                re.append(a)
                im.append(b)
            re, im = dft8(re, im, 1)
            for al in range(8):
                a, b = cmul(re[al], im[al], tw[al, 0, rows, ln], -tw[al, 1, rows, ln])
                if last:
                    ce[al, :, ln] = a[0:8]
                else:
                    mark = top[:, 0:128] * (even * (r == 6).astype(F32))
                    head = b[0:8] * (1.0 - mark) + ce[al, 0:1, ln] * mark
                    b = jnp.concatenate([head, b[8:16]], 0)
                    down = pl.ds(pl.multiple_of(128 + r * 16, 16), 16)
                    ch[al, rows, ln], cl[al, rows, ln] = split(a)
                    ch[al, down, ln], cl[al, down, ln] = split(b)

    back(8, True)
    loop(8, lambda r: back(r, False))

    def combine(k, dst):
        rows = pl.ds(pl.multiple_of(k * 128, 128), 128)

        def body(al):
            vh, vl = m256v[2, rows, :], m256v[3, rows, :]
            y = dot(vh, ch[al]) + dot(vh, cl[al]) + dot(vl, ch[al])
            dst[pl.ds(2 * al, 128, stride=16), :] = y[:, 0:128]
            dst[pl.ds(2 * al + 1, 128, stride=16), :] = y[:, 128:256]

        loop(8, body)

    combine(other, yo)
    swap = remote(yo, pb, 4, chip, other)
    swap.start()
    combine(core, yw)
    pltpu.make_async_copy(pb, pb, rsem.at[4]).wait()

    def rows_of(t):
        return pl.ds(pl.multiple_of(t * 16, 16), 16)

    def send_out(i):
        t = lax.rem(chip + i, 128)
        ys[rows_of(t), :] = yw[rows_of(t), :] + pb[rows_of(t), :]
        remote(ys.at[rows_of(t)], yb.at[rows_of(chip)], 5, t, core).start()

    loop(128, send_out, 1)
    ys[rows_of(chip), :] = yw[rows_of(chip), :] + pb[rows_of(chip), :]
    pltpu.make_async_copy(ys.at[rows_of(chip)], yb.at[rows_of(chip)], rsem.at[5]).start()
    pltpu.make_async_copy(yb, yb, rsem.at[5]).wait()

    def finish(a):
        rows = pl.ds(pl.multiple_of(a * 128, 128), 128)
        conv = yb[pl.ds(a, 128, stride=16), :].T
        value = conv + skip[...] * sig[rows, :].astype(F32)
        out[rows, :] = (gv[rows, :].astype(F32) * value).astype(BF16)

    loop(16, finish)

    def sent(ref, sem):
        pltpu.make_async_copy(ref, ref, ssem.at[sem]).wait()

    sent(xs.at[pl.ds(0, 127)], 0)
    sent(fs.at[pl.ds(0, 255)], 1)

    @pl.when(here == 0)
    def _():
        sent(es.at[pl.ds(0, 127)], 2)

    forward.wait_send()
    swap.wait_send()
    sent(ys.at[pl.ds(0, 127 * 16)], 5)


def body(signal, gate, filters, skip):
    m256, m512, tb, ta, t2 = (jnp.asarray(t) for t in tables())
    vmem = pl.BlockSpec(memory_space=pltpu.VMEM)
    hbm = pl.BlockSpec(memory_space=pl.ANY)
    return pl.pallas_call(
        kernel,
        out_shape=jax.ShapeDtypeStruct(signal.shape, BF16),
        in_specs=[vmem, hbm, hbm, vmem, hbm, hbm, hbm, hbm, hbm],
        out_specs=vmem,
        scratch_shapes=[
            pltpu.VMEM((2, 8, 256, 128), BF16),
            pltpu.VMEM((2, 1, 256, 128), BF16),
            pltpu.VMEM((2048, 128), BF16),
            pltpu.VMEM((4, 256, 256), BF16),
            pltpu.VMEM((4, 512, 512), BF16),
            pltpu.VMEM((2, ROWS, 256), F32),
            pltpu.VMEM((ROWS, 128), F32),
            pltpu.VMEM((2, 8, 256), F32),
            pltpu.VMEM((2048, 128), F32),
            pltpu.VMEM((128, 16, 128), BF16),
            pltpu.VMEM((256, 16, 128), BF16),
            pltpu.VMEM((4096, 128), F32),
            pltpu.VMEM((256, 16, 128), BF16),
            pltpu.VMEM((128, 16, 128), BF16),
            pltpu.VMEM((256, 16, 128), BF16),
            pltpu.VMEM((1, 16, 128), BF16),
            pltpu.VMEM((8, 2, ROWS, 256), F32),
            pltpu.VMEM((8, 2, ROWS, 256), F32),
            pltpu.VMEM((8, 2, ROWS, 256), F32),
            pltpu.VMEM((8, ROWS, 512), BF16),
            pltpu.VMEM((8, ROWS, 512), BF16),
            pltpu.VMEM((8, ROWS, 512), F32),
            pltpu.VMEM((8, 8, 256), F32),
            pltpu.VMEM((8, 256, 256), BF16),
            pltpu.VMEM((8, 256, 256), BF16),
            pltpu.VMEM((2048, 128), F32),
            pltpu.VMEM((2048, 128), F32),
            pltpu.VMEM((2048, 128), F32),
            pltpu.VMEM((2048, 128), F32),
            pltpu.VMEM((2048, 128), F32),
            pltpu.SemaphoreType.DMA((8,)),
            pltpu.SemaphoreType.DMA((6,)),
            pltpu.SemaphoreType.DMA((6,)),
        ],
        compiler_params=pltpu.CompilerParams(
            collective_id=0, has_side_effects=True, vmem_limit_bytes=56 << 20
        ),
    )(signal, filters, gate, skip[None, :], m256, m512, tb, ta, t2)


def solution(mesh):
    placed = (
        P(("ctx", "cp"), None),
        P(("ctx", "cp"), None),
        P(None, ("ctx", "cp"), None, None),
        P(),
    )
    return jax.shard_map(
        body, mesh=mesh, in_specs=placed, out_specs=P(("ctx", "cp"), None), check_vma=False
    )
```

time: 594 us -> 97.9 us (0.16); the launches traced: 582 us -> 97.7 us
  blocking collectives: 195 us -> 0 us
  local copies, waits for them, and re-layouts: 143 us -> 1.87 us
  waiting for transfers between devices: 117 us -> 0 us
  Pallas kernels: 0 us -> 95.8 us
  matrix products: 63.8 us -> 0 us
  other arithmetic: 43.7 us -> 0 us
  starting transfers between devices: 18.6 us -> 0 us
    all_to_all x5 -> x0, blocking collectives: 195 us -> none  [the longest x1 52.8 us: body(): lax.all_to_all(jnp.stack([back_re, back_im]), 'ctx', split_axis=2, concat...]
    all_to_all x3 -> x0, waiting for transfers between devices: 117 us -> none  [the longest x1 51.9 us: body(): lax.all_to_all(lax.all_to_all(jnp.stack([back_re, back_im]), 'ctx', split...]
    pallas_call x0 -> x1, Pallas kernels: none -> 95.8 us  [body(): pl.pallas_call(kernel, out_shape=jax.ShapeDtypeStruct(signal.shape, BF16)...]
    dot_general x22 -> x0, matrix products: 63.8 us -> none  [the longest x4 13.3 us: complex_apply(): jnp.einsum(form, mat_re, val_re, precision=HIGHEST)]
    unnamed x45 -> x1, local copies, waits for them, and re-layouts: 50.9 us -> 1.87 us
    all_to_all x9 -> x0, local copies, waits for them, and re-layouts: 24.4 us -> none  [the longest x2 10.3 us: body(): lax.all_to_all(jnp.stack([back_re, back_im]), 'ctx', split_axis=2, concat...]
    all_to_all x3 -> x0, other arithmetic: 21.9 us -> none  [the longest x1 7.37 us: body(): lax.all_to_all(jnp.stack([back_re, back_im]), 'ctx', split_axis=2, concat...]
    all_to_all x3 -> x0, starting transfers between devices: 18.6 us -> none  [the longest x1 8.23 us: body(): lax.all_to_all(lax.all_to_all(local, 'ctx', split_axis=1, concat_axis=0,...]
  transfers between devices with their start and end apart: 3 -> 0, of which waited for: 3 -> 0; matrix products, arithmetic and copies ran while one was open for 1% -> 0% of each run, Pallas kernels for 0% -> 0%
where the time goes in v1:
time: 97.9 us; the launch traced here: 97.7 us
  Pallas kernels  95.8 us (98%)
  local copies, waits for them, and re-layouts  1.87 us (2%)
    pallas_call x1, Pallas kernels, body(): pl.pallas_call(kernel, out_shape=jax.ShapeDtypeStruct(signal.shape, BF16)...  95.8 us

profile of v1, /device:TPU:32, one launch (start us, length us, event | category | flops | bytes accessed | tf_op | source)
XLA Modules:
  0.0 97.7 jit_solution(9663600974317108751)
XLA Ops:
  0.0 95.8 %shard_map.91 = bf16[2048,128]{1,0:T(8,128)(2,1)} custom-call(bf16[2048,128]{1,0:T(8,128)(2,1)} %sig.1, bf16[2,16,256,128]{3,2,1,0:T(8,128)(2,1)} %filt.1, bf16[2048,128]{1,0:T(8,128)(2,1)} %gate.1, f32[1,128]{1,0:T(1,128)} %bitcast.1, bf16[2,4,256,256]{3,2,1,0:T(8,128)(2,1)} %constant.10.clone.m256, bf16[4,512,512]{2,1,0:T(8,128)(2,1)} %constant.11.clone.m512, ...), custom_call_target="tpu_custom_call" | custom-call | tf_op jit(solution)/shard_map/pallas_call | solution.py:464
  95.9 1.9 %copy.11 = bf16[2048,128]{1,0:T(8,128)(2,1)} copy(bf16[2048,128]{1,0:T(8,128)(2,1)} %shard_map.91) | data formatting | bytes 1048576

commit v2 on v1

--- a/solution.py
+++ b/solution.py
@@ -12,6 +12,7 @@
 
 
 FULL = 1 << 20
+SPAN = 2.0**7.75
 ROWS = 144
 F32 = jnp.float32
 BF16 = jnp.bfloat16
@@ -64,12 +65,7 @@
         cos, sin = phase(sigma[:, None] * al[None, :], 4096)
         ta[core, :129, 0:8], ta[core, :129, 8:16] = cos, -sin
     cos, sin = phase(beta[:, None] * beta[None, :], 256)
-    m512 = np.stack(
-        [
-            *split_np(np.block([[cos, -sin], [sin, cos]])),
-            *split_np(np.block([[cos, sin], [-sin, cos]])),
-        ]
-    )
+    m512 = np.stack(split_np(np.block([[cos, -sin], [sin, cos]])))
     cos, sin = phase(al[:, None] * beta[None, :], 2048)
     t2 = np.stack([cos, -sin]).astype(np.float32)
     return np.stack(m256), m512, tb, ta, t2
@@ -123,11 +119,15 @@
     return jnp.dot(a, b, preferred_element_type=F32)
 
 
+def dot_t(a, b):
+    return lax.dot_general(a, b, (((1,), (1,)), ((), ())), preferred_element_type=F32)
+
+
 def kernel(
     sig, filt, gate, skip, m256, m512, tb, ta, t2, out,
     fv, ev, gv, m256v, m512v, tbv, tav, t2v,
     s32, xs, xb, x32, fs, es, hb, eb, hf, fz, tw, zh, zl, gg, ce, ch, cl,
-    yo, yw, ys, pb, yb, lsem, ssem, rsem,
+    yo, yw, pb, ye, yb, se, sb, lsem, ssem, rsem,
 ):
     ctx, cp = lax.axis_index("ctx"), lax.axis_index("cp")
     core = lax.rem(ctx, 2)
@@ -318,16 +318,16 @@
 
     loop(9, second)
 
-    def third(base):
+    def third(mul):
         def body(j):
             a = zh[pl.ds(j * 2, 2)].reshape(2 * ROWS, 512)
             b = zl[pl.ds(j * 2, 2)].reshape(2 * ROWS, 512)
-            g = dot(a, m512v[base]) + dot(a, m512v[base + 1]) + dot(b, m512v[base])
+            g = mul(a, m512v[0]) + mul(a, m512v[1]) + mul(b, m512v[0])
             gg[pl.ds(j * 2, 2)] = g.reshape(2, ROWS, 512)
 
         loop(4, body)
 
-    third(0)
+    third(dot)
 
     pltpu.make_async_copy(hb, hb, rsem.at[1]).wait()
     widen(hb, x32)
@@ -374,7 +374,7 @@
         loop(9, body)
 
     loop(8, apply_filter)
-    third(2)
+    third(dot_t)
 
     def back(r, last):
         rows = pl.ds(r * 16, 16) if last else pl.ds(pl.multiple_of(r * 16, 16), 16)
@@ -421,25 +421,63 @@
     combine(core, yw)
     pltpu.make_async_copy(pb, pb, rsem.at[4]).wait()
 
-    def rows_of(t):
-        return pl.ds(pl.multiple_of(t * 16, 16), 16)
+    weight = skip[chip]
+
+    def add_up(i, peak):
+        rows = pl.ds(pl.multiple_of(i * 128, 128), 128)
+        x = xb[pl.ds(core * 128 + i * 8, 8)].astype(F32).reshape(128, 128)
+        value = yw[rows, :] + pb[rows, :] + weight * x
+        yw[rows, :] = value
+        size = jnp.abs(value).reshape(16, 8, 128)
+        return jnp.maximum(peak, jnp.max(size, axis=0))
+
+    peak = lax.fori_loop(0, 16, add_up, jnp.zeros((8, 128), F32))
+    peak = jnp.max(jnp.max(peak, axis=1, keepdims=True), axis=0, keepdims=True)
+    peak = jnp.maximum(jnp.broadcast_to(peak, (1, 128)), 2.0**-118)
+    se[0] = peak * (1.0 / SPAN)
+    shrink = SPAN / peak
+
+    def encode(i):
+        rows = pl.ds(pl.multiple_of(i * 128, 128), 128)
+        value = yw[rows, :] * shrink
+        power = value * value
+        power = power * power
+        power = power * power
+        power = power * power
+        code = jnp.where(value < 0, -power, power)
+        ye[pl.ds(i * 8, 8)] = code.astype(BF16).reshape(8, 16, 128)
+
+    loop(16, encode)
 
     def send_out(i):
         t = lax.rem(chip + i, 128)
-        ys[rows_of(t), :] = yw[rows_of(t), :] + pb[rows_of(t), :]
-        remote(ys.at[rows_of(t)], yb.at[rows_of(chip)], 5, t, core).start()
-
+        remote(ye.at[t], yb.at[chip], 5, t, core).start()
+
+    def send_scale(i):
+        t = lax.rem(chip + i, 128)
+        remote(se.at[0], sb.at[chip], 6, t, core).start()
+
+    pltpu.make_async_copy(ye.at[chip], yb.at[chip], rsem.at[5]).start()
+    pltpu.make_async_copy(se.at[0], sb.at[chip], rsem.at[6]).start()
     loop(128, send_out, 1)
-    ys[rows_of(chip), :] = yw[rows_of(chip), :] + pb[rows_of(chip), :]
-    pltpu.make_async_copy(ys.at[rows_of(chip)], yb.at[rows_of(chip)], rsem.at[5]).start()
+    loop(128, send_scale, 1)
+    pltpu.make_async_copy(sb, sb, rsem.at[6]).wait()
     pltpu.make_async_copy(yb, yb, rsem.at[5]).wait()
+
+    def decode(i):
+        for j in range(8):
+            code = yb[i * 8 + j].astype(F32)
+            size = jnp.exp2(jnp.log2(jnp.abs(code)) * (1.0 / 16)) * sb[i * 8 + j]
+            rows = pl.ds(pl.multiple_of(i * 128 + j * 16, 16), 16)
+            yo[rows, :] = jnp.where(code < 0, -size, size)
 
     def finish(a):
         rows = pl.ds(pl.multiple_of(a * 128, 128), 128)
-        conv = yb[pl.ds(a, 128, stride=16), :].T
-        value = conv + skip[...] * sig[rows, :].astype(F32)
+        value = yo[pl.ds(a, 128, stride=16), :].T
         out[rows, :] = (gv[rows, :].astype(F32) * value).astype(BF16)
 
+    swap.wait_send()
+    loop(16, decode)
     loop(16, finish)
 
     def sent(ref, sem):
@@ -453,25 +491,26 @@
         sent(es.at[pl.ds(0, 127)], 2)
 
     forward.wait_send()
-    swap.wait_send()
-    sent(ys.at[pl.ds(0, 127 * 16)], 5)
+    sent(ye.at[pl.ds(0, 127)], 5)
+    sent(sb.at[pl.ds(0, 127)], 6)
 
 
 def body(signal, gate, filters, skip):
     m256, m512, tb, ta, t2 = (jnp.asarray(t) for t in tables())
     vmem = pl.BlockSpec(memory_space=pltpu.VMEM)
     hbm = pl.BlockSpec(memory_space=pl.ANY)
+    smem = pl.BlockSpec(memory_space=pltpu.SMEM)
     return pl.pallas_call(
         kernel,
         out_shape=jax.ShapeDtypeStruct(signal.shape, BF16),
-        in_specs=[vmem, hbm, hbm, vmem, hbm, hbm, hbm, hbm, hbm],
+        in_specs=[vmem, hbm, hbm, smem, hbm, hbm, hbm, hbm, hbm],
         out_specs=vmem,
         scratch_shapes=[
             pltpu.VMEM((2, 8, 256, 128), BF16),
             pltpu.VMEM((2, 1, 256, 128), BF16),
             pltpu.VMEM((2048, 128), BF16),
             pltpu.VMEM((4, 256, 256), BF16),
-            pltpu.VMEM((4, 512, 512), BF16),
+            pltpu.VMEM((2, 512, 512), BF16),
             pltpu.VMEM((2, ROWS, 256), F32),
             pltpu.VMEM((ROWS, 128), F32),
             pltpu.VMEM((2, 8, 256), F32),
@@ -495,16 +534,18 @@
             pltpu.VMEM((2048, 128), F32),
             pltpu.VMEM((2048, 128), F32),
             pltpu.VMEM((2048, 128), F32),
-            pltpu.VMEM((2048, 128), F32),
-            pltpu.VMEM((2048, 128), F32),
+            pltpu.VMEM((128, 16, 128), BF16),
+            pltpu.VMEM((128, 16, 128), BF16),
+            pltpu.VMEM((1, 1, 128), F32),
+            pltpu.VMEM((128, 1, 128), F32),
             pltpu.SemaphoreType.DMA((8,)),
-            pltpu.SemaphoreType.DMA((6,)),
-            pltpu.SemaphoreType.DMA((6,)),
+            pltpu.SemaphoreType.DMA((7,)),
+            pltpu.SemaphoreType.DMA((7,)),
         ],
         compiler_params=pltpu.CompilerParams(
             collective_id=0, has_side_effects=True, vmem_limit_bytes=56 << 20
         ),
-    )(signal, filters, gate, skip[None, :], m256, m512, tb, ta, t2)
+    )(signal, filters, gate, skip, m256, m512, tb, ta, t2)
 
 
 def solution(mesh):

time: 97.9 us -> 93.4 us (0.954); the launches traced: 97.7 us -> 91.8 us
  Pallas kernels: 95.8 us -> 89.9 us
    pallas_call x1, Pallas kernels: 95.8 us -> 89.9 us  [body(): pl.pallas_call(kernel, out_shape=jax.ShapeDtypeStruct(signal.shape, BF16)...]
where the time goes in v2:
time: 93.4 us; the launch traced here: 91.8 us
  Pallas kernels  89.9 us (96%)
  local copies, waits for them, and re-layouts  1.87 us (2%)
    pallas_call x1, Pallas kernels, body(): pl.pallas_call(kernel, out_shape=jax.ShapeDtypeStruct(signal.shape, BF16)...  89.9 us
    unnamed x1, local copies, waits for them, and re-layouts  1.87 us

profile of v2, /device:TPU:32, one launch (start us, length us, event | category | flops | bytes accessed | tf_op | source)
XLA Modules:
  0.0 91.8 jit_solution(4154610157563530541)
XLA Ops:
  0.0 89.9 %shard_map.91 = bf16[2048,128]{1,0:T(8,128)(2,1)} custom-call(bf16[2048,128]{1,0:T(8,128)(2,1)} %sig.1, bf16[2,16,256,128]{3,2,1,0:T(8,128)(2,1)} %filt.1, bf16[2048,128]{1,0:T(8,128)(2,1)} %gate.1, f32[128]{0:T(128)} %skip.1, bf16[2,4,256,256]{3,2,1,0:T(8,128)(2,1)} %constant.10.clone.m256, bf16[2,512,512]{2,1,0:T(8,128)(2,1)} %constant.11.clone.m512, ...), custom_call_target="tpu_custom_call" | custom-call | tf_op jit(solution)/shard_map/pallas_call | solution.py:503
  89.9 1.9 %copy.11 = bf16[2048,128]{1,0:T(8,128)(2,1)} copy(bf16[2048,128]{1,0:T(8,128)(2,1)} %shard_map.91) | data formatting | bytes 1048576

commit v3 on v2

--- a/solution.py
+++ b/solution.py
@@ -58,7 +58,7 @@
             nyquist = phase(256 * block, 512)[0]
             fwd[128 + 96] = nyquist
             inv[:, 128 + 96] = nyquist
-        inv = inv * (2.0 / FULL)
+        inv = np.roll(inv, 128 * core - 128, axis=0) * (2.0 / FULL)
         m256.append(np.stack([*split_np(fwd), *split_np(inv)]))
         cos, sin = phase(sigma[:, None] * beta[None, :], FULL)
         tb[core, 0, :129], tb[core, 1, :129] = cos, -sin
@@ -127,7 +127,7 @@
     sig, filt, gate, skip, m256, m512, tb, ta, t2, out,
     fv, ev, gv, m256v, m512v, tbv, tav, t2v,
     s32, xs, xb, x32, fs, es, hb, eb, hf, fz, tw, zh, zl, gg, ce, ch, cl,
-    yo, yw, pb, ye, yb, se, sb, lsem, ssem, rsem,
+    yo, yw, pb, v32, h32, ye, yb, se, sb, lsem, ssem, rsem, swap_s, swap_r,
 ):
     ctx, cp = lax.axis_index("ctx"), lax.axis_index("cp")
     core = lax.rem(ctx, 2)
@@ -330,7 +330,7 @@
     third(dot)
 
     pltpu.make_async_copy(hb, hb, rsem.at[1]).wait()
-    widen(hb, x32)
+    widen(hb, h32)
 
     def place_filter(e, shift):
         for ri in range(2):
@@ -341,7 +341,7 @@
                 lo = blk * 32 + (1 if shift and blk == 3 else 0)
                 for qh in range(2):
                     start = e * 512 + (ri * 8 + blk * 2 + qh)
-                    hf[e, ri, lo : lo + 32, qh * 128 : qh * 128 + 128] = x32[
+                    hf[e, ri, lo : lo + 32, qh * 128 : qh * 128 + 128] = h32[
                         pl.ds(start, 32, stride=16), :
                     ]
 
@@ -404,34 +404,34 @@
     back(8, True)
     loop(8, lambda r: back(r, False))
 
-    def combine(k, dst):
-        rows = pl.ds(pl.multiple_of(k * 128, 128), 128)
-
-        def body(al):
-            vh, vl = m256v[2, rows, :], m256v[3, rows, :]
-            y = dot(vh, ch[al]) + dot(vh, cl[al]) + dot(vl, ch[al])
-            dst[pl.ds(2 * al, 128, stride=16), :] = y[:, 0:128]
-            dst[pl.ds(2 * al + 1, 128, stride=16), :] = y[:, 128:256]
-
-        loop(8, body)
-
-    combine(other, yo)
-    swap = remote(yo, pb, 4, chip, other)
-    swap.start()
-    combine(core, yw)
-    pltpu.make_async_copy(pb, pb, rsem.at[4]).wait()
+    def swap(al):
+        return pltpu.make_async_remote_copy(
+            src_ref=yo.at[al], dst_ref=pb.at[al], send_sem=swap_s.at[al], recv_sem=swap_r.at[al],
+            device_id=device(chip, other), device_id_type=pl.DeviceIdType.MESH,
+        )
+
+    def combine(al):
+        vh, vl = m256v[2], m256v[3]
+        y = dot(vh, ch[al]) + dot(vh, cl[al]) + dot(vl, ch[al])
+        yo[al] = y[0:128]
+        swap(al).start()
+        yw[al] = y[128:256]
+
+    loop(8, combine)
 
     weight = skip[chip]
 
-    def add_up(i, peak):
-        rows = pl.ds(pl.multiple_of(i * 128, 128), 128)
-        x = xb[pl.ds(core * 128 + i * 8, 8)].astype(F32).reshape(128, 128)
-        value = yw[rows, :] + pb[rows, :] + weight * x
-        yw[rows, :] = value
-        size = jnp.abs(value).reshape(16, 8, 128)
-        return jnp.maximum(peak, jnp.max(size, axis=0))
-
-    peak = lax.fori_loop(0, 16, add_up, jnp.zeros((8, 128), F32))
+    def add_up(al, peak):
+        swap(al).wait()
+        for half in range(2):
+            ln = slice(half * 128, half * 128 + 128)
+            x = x32[pl.ds(core * 2048 + 2 * al + half, 128, stride=16), :]
+            value = yw[al, :, ln] + pb[al, :, ln] + weight * x
+            v32[pl.ds(2 * al + half, 128, stride=16), :] = value
+            peak = jnp.maximum(peak, jnp.max(jnp.abs(value).reshape(16, 8, 128), axis=0))
+        return peak
+
+    peak = lax.fori_loop(0, 8, add_up, jnp.zeros((8, 128), F32))
     peak = jnp.max(jnp.max(peak, axis=1, keepdims=True), axis=0, keepdims=True)
     peak = jnp.maximum(jnp.broadcast_to(peak, (1, 128)), 2.0**-118)
     se[0] = peak * (1.0 / SPAN)
@@ -439,7 +439,7 @@
 
     def encode(i):
         rows = pl.ds(pl.multiple_of(i * 128, 128), 128)
-        value = yw[rows, :] * shrink
+        value = v32[rows, :] * shrink
         power = value * value
         power = power * power
         power = power * power
@@ -467,16 +467,16 @@
     def decode(i):
         for j in range(8):
             code = yb[i * 8 + j].astype(F32)
-            size = jnp.exp2(jnp.log2(jnp.abs(code)) * (1.0 / 16)) * sb[i * 8 + j]
+            size = jnp.maximum(jnp.abs(code), 2.0**-126)
+            size = lax.rsqrt(lax.rsqrt(lax.rsqrt(lax.rsqrt(size)))) * sb[i * 8 + j]
             rows = pl.ds(pl.multiple_of(i * 128 + j * 16, 16), 16)
-            yo[rows, :] = jnp.where(code < 0, -size, size)
+            s32[rows, :] = jnp.where(code < 0, -size, size)
 
     def finish(a):
         rows = pl.ds(pl.multiple_of(a * 128, 128), 128)
-        value = yo[pl.ds(a, 128, stride=16), :].T
+        value = s32[pl.ds(a, 128, stride=16), :].T
         out[rows, :] = (gv[rows, :].astype(F32) * value).astype(BF16)
 
-    swap.wait_send()
     loop(16, decode)
     loop(16, finish)
 
@@ -531,9 +531,11 @@
             pltpu.VMEM((8, 8, 256), F32),
             pltpu.VMEM((8, 256, 256), BF16),
             pltpu.VMEM((8, 256, 256), BF16),
+            pltpu.VMEM((8, 128, 256), F32),
+            pltpu.VMEM((8, 128, 256), F32),
+            pltpu.VMEM((8, 128, 256), F32),
             pltpu.VMEM((2048, 128), F32),
-            pltpu.VMEM((2048, 128), F32),
-            pltpu.VMEM((2048, 128), F32),
+            pltpu.VMEM((4096, 128), F32),
             pltpu.VMEM((128, 16, 128), BF16),
             pltpu.VMEM((128, 16, 128), BF16),
             pltpu.VMEM((1, 1, 128), F32),
@@ -541,6 +543,8 @@
             pltpu.SemaphoreType.DMA((8,)),
             pltpu.SemaphoreType.DMA((7,)),
             pltpu.SemaphoreType.DMA((7,)),
+            pltpu.SemaphoreType.DMA((8,)),
+            pltpu.SemaphoreType.DMA((8,)),
         ],
         compiler_params=pltpu.CompilerParams(
             collective_id=0, has_side_effects=True, vmem_limit_bytes=56 << 20

time: 93.4 us -> 92.4 us (0.989)
  no operation moved by 1% of the time
where the time goes in v3:
time: 92.4 us; the launch traced here: 91.1 us
  Pallas kernels  89.2 us (97%)
  local copies, waits for them, and re-layouts  1.87 us (2%)
    pallas_call x1, Pallas kernels, body(): pl.pallas_call(kernel, out_shape=jax.ShapeDtypeStruct(signal.shape, BF16)...  89.2 us
    unnamed x1, local copies, waits for them, and re-layouts  1.87 us

profile of v3, /device:TPU:32, one launch (start us, length us, event | category | flops | bytes accessed | tf_op | source)
XLA Modules:
  0.0 91.1 jit_solution(4573899427507211450)
XLA Ops:
  0.0 89.2 %shard_map.91 = bf16[2048,128]{1,0:T(8,128)(2,1)} custom-call(bf16[2048,128]{1,0:T(8,128)(2,1)} %sig.1, bf16[2,16,256,128]{3,2,1,0:T(8,128)(2,1)} %filt.1, bf16[2048,128]{1,0:T(8,128)(2,1)} %gate.1, f32[128]{0:T(128)} %skip.1, bf16[2,4,256,256]{3,2,1,0:T(8,128)(2,1)} %constant.10.clone.m256, bf16[2,512,512]{2,1,0:T(8,128)(2,1)} %constant.11.clone.m512, ...), custom_call_target="tpu_custom_call" | custom-call | tf_op jit(solution)/shard_map/pallas_call | solution.py:503
  89.2 1.9 %copy.11 = bf16[2048,128]{1,0:T(8,128)(2,1)} copy(bf16[2048,128]{1,0:T(8,128)(2,1)} %shard_map.91) | data formatting | bytes 1048576

commit v4 on v3

--- a/solution.py
+++ b/solution.py
@@ -126,7 +126,7 @@
 def kernel(
     sig, filt, gate, skip, m256, m512, tb, ta, t2, out,
     fv, ev, gv, m256v, m512v, tbv, tav, t2v,
-    s32, xs, xb, x32, fs, es, hb, eb, hf, fz, tw, zh, zl, gg, ce, ch, cl,
+    s32, xs, xb, x32, fs, hb, hf, fz, tw, zh, zl, gg, ce, ch, cl,
     yo, yw, pb, v32, h32, ye, yb, se, sb, lsem, ssem, rsem, swap_s, swap_r,
 ):
     ctx, cp = lax.axis_index("ctx"), lax.axis_index("cp")
@@ -166,7 +166,7 @@
     upper = (place >= 32).astype(jnp.int32)
     loads = [
         pltpu.make_async_copy(filt.at[:, pl.ds(upper * 8, 8)], fv, lsem.at[0]),
-        pltpu.make_async_copy(filt.at[:, pl.ds(8, 1)], ev, lsem.at[1]),
+        pltpu.make_async_copy(filt.at[:, pl.ds(8, 1), pl.ds(0, 128)], ev, lsem.at[1]),
         pltpu.make_async_copy(ta.at[core], tav, lsem.at[2]),
         pltpu.make_async_copy(tb.at[core], tbv, lsem.at[3]),
         pltpu.make_async_copy(m256.at[core], m256v, lsem.at[4]),
@@ -206,20 +206,19 @@
 
             loop(4, body)
 
-    for k in range(2):
-        turn_filter(k)
-        pack(fs, k * 128)
-
-    @pl.when(here == 0)
-    def _():
-        def body(j):
-            ri, qh = j // 2, lax.rem(j, 2)
-            block = ev[ri, 0, pl.ds(pl.multiple_of(qh * 128, 128), 128), :].astype(F32).T
-            for blk in range(4):
-                s32[pl.ds(ri * 8 + blk * 2 + qh, 128, stride=16), :] = block
-
-        loop(4, body)
-        pack(es, 0)
+    def pack_mirrors():
+        for ri in range(2):
+            s32[pl.ds(ri * 8 + 7, 128, stride=16), :] = ev[ri, 0].astype(F32).T
+        head = lax.broadcasted_iota(jnp.int32, (128, 128), 0) == 0
+        middle = fv[0, 0, 128:136, :].astype(F32)[0:1]
+        block = jnp.where(head, middle, fv[1, 0, 0:128, :].astype(F32))
+        s32[pl.ds(8 + 6, 128, stride=16), :] = block.T
+
+    turn_filter(0)
+    pl.when(here == 0)(pack_mirrors)
+    pack(fs, 0)
+    turn_filter(1)
+    pack(fs, 128)
 
     loads[2].wait()
     loads[3].wait()
@@ -254,14 +253,6 @@
     pltpu.make_async_copy(fs.at[core * 128 + chip], hb.at[fslot], rsem.at[1]).start()
     remote(fs.at[other * 128 + chip], hb.at[fslot], 1, chip, other).start()
     loop(128, send_filter, 1)
-
-    @pl.when(here == 0)
-    def _():
-        def body(t):
-            remote(es.at[t], eb.at[0], 2, t, 0).start()
-
-        pltpu.make_async_copy(es.at[0], eb.at[0], rsem.at[2]).start()
-        loop(128, body, 1)
 
     mine = xb.at[pl.ds(core * 128, 128)]
     theirs = xb.at[pl.ds(other * 128, 128)]
@@ -354,13 +345,14 @@
     @pl.when(core == 0)
     def _():
         loop(8, lambda e: place_filter(e, True), 4)
-        pltpu.make_async_copy(eb, eb, rsem.at[2]).wait()
-        extra = eb[0].astype(F32)
+        lane = (lax.broadcasted_iota(jnp.int32, (1, 128), 1) == 0).astype(F32)
+        re, im = hf[0, 0, 96:97, 0:128], hf[0, 1, 96:97, 0:128]
         for ri in range(2):
-            hf[0, ri, 96:97, :] = hf[0, ri, 96:97, :] * 0.5
-            for qh in range(2):
-                row = ri * 8 + 6 + qh
-                hf[4, ri, 96:97, qh * 128 : qh * 128 + 128] = extra[row : row + 1] * 0.5
+            hf[4, ri, 96:97, 0:128] = hf[0, ri, 96:97, 128:256]
+        hf[0, 0, 96:97, 0:128] = re * (1.0 - 0.5 * lane)
+        hf[0, 1, 96:97, 0:128] = im * (1.0 - lane)
+        hf[0, 0, 96:97, 128:256] = im * (0.5 * lane)
+        hf[0, 1, 96:97, 128:256] = jnp.zeros((1, 128), F32)
 
     def apply_filter(e):
         def body(r):
@@ -486,10 +478,6 @@
     sent(xs.at[pl.ds(0, 127)], 0)
     sent(fs.at[pl.ds(0, 255)], 1)
 
-    @pl.when(here == 0)
-    def _():
-        sent(es.at[pl.ds(0, 127)], 2)
-
     forward.wait_send()
     sent(ye.at[pl.ds(0, 127)], 5)
     sent(sb.at[pl.ds(0, 127)], 6)
@@ -507,7 +495,7 @@
         out_specs=vmem,
         scratch_shapes=[
             pltpu.VMEM((2, 8, 256, 128), BF16),
-            pltpu.VMEM((2, 1, 256, 128), BF16),
+            pltpu.VMEM((2, 1, 128, 128), BF16),
             pltpu.VMEM((2048, 128), BF16),
             pltpu.VMEM((4, 256, 256), BF16),
             pltpu.VMEM((2, 512, 512), BF16),
@@ -519,9 +507,7 @@
             pltpu.VMEM((256, 16, 128), BF16),
             pltpu.VMEM((4096, 128), F32),
             pltpu.VMEM((256, 16, 128), BF16),
-            pltpu.VMEM((128, 16, 128), BF16),
             pltpu.VMEM((256, 16, 128), BF16),
-            pltpu.VMEM((1, 16, 128), BF16),
             pltpu.VMEM((8, 2, ROWS, 256), F32),
             pltpu.VMEM((8, 2, ROWS, 256), F32),
             pltpu.VMEM((8, 2, ROWS, 256), F32),

time: 92.4 us -> 91.8 us (level)
  no operation moved by 1% of the time
where the time goes in v4:
time: 91.8 us; the launch traced here: 90.5 us
  Pallas kernels  88.6 us (97%)
  local copies, waits for them, and re-layouts  1.87 us (2%)
    pallas_call x1, Pallas kernels, body(): pl.pallas_call(kernel, out_shape=jax.ShapeDtypeStruct(signal.shape, BF16)...  88.6 us
    unnamed x1, local copies, waits for them, and re-layouts  1.87 us

profile of v4, /device:TPU:32, one launch (start us, length us, event | category | flops | bytes accessed | tf_op | source)
XLA Modules:
  0.0 90.5 jit_solution(10851053847931304308)
XLA Ops:
  0.0 88.6 %shard_map.91 = bf16[2048,128]{1,0:T(8,128)(2,1)} custom-call(bf16[2048,128]{1,0:T(8,128)(2,1)} %sig.1, bf16[2,16,256,128]{3,2,1,0:T(8,128)(2,1)} %filt.1, bf16[2048,128]{1,0:T(8,128)(2,1)} %gate.1, f32[128]{0:T(128)} %skip.1, bf16[2,4,256,256]{3,2,1,0:T(8,128)(2,1)} %constant.10.clone.m256, bf16[2,512,512]{2,1,0:T(8,128)(2,1)} %constant.11.clone.m512, ...), custom_call_target="tpu_custom_call" | custom-call | tf_op jit(solution)/shard_map/pallas_call | solution.py:491
  88.6 1.9 %copy.11 = bf16[2048,128]{1,0:T(8,128)(2,1)} copy(bf16[2048,128]{1,0:T(8,128)(2,1)} %shard_map.91) | data formatting | bytes 1048576

commit v5 on v4

--- a/solution.py
+++ b/solution.py
@@ -119,6 +119,10 @@
     return jnp.dot(a, b, preferred_element_type=F32)
 
 
+def slot_of(e):
+    return 2 * e if e < 4 else 2 * (7 - e) + 1
+
+
 def dot_t(a, b):
     return lax.dot_general(a, b, (((1,), (1,)), ((), ())), preferred_element_type=F32)
 
@@ -126,8 +130,8 @@
 def kernel(
     sig, filt, gate, skip, m256, m512, tb, ta, t2, out,
     fv, ev, gv, m256v, m512v, tbv, tav, t2v,
-    s32, xs, xb, x32, fs, hb, hf, fz, tw, zh, zl, gg, ce, ch, cl,
-    yo, yw, pb, v32, h32, ye, yb, se, sb, lsem, ssem, rsem, swap_s, swap_r,
+    s32, xs, xb, x32, fs, hb, hf, fz, tw, zh, zl, gg, keep, ce, ch, cl,
+    yo, yw, pb, v32, h32, ye, yb, se, sb, lsem, ssem, rsem, swap_s, swap_r, wave_r,
 ):
     ctx, cp = lax.axis_index("ctx"), lax.axis_index("cp")
     core = lax.rem(ctx, 2)
@@ -243,16 +247,25 @@
     pltpu.make_async_copy(xs.at[chip], xb.at[slot], rsem.at[0]).start()
     loop(128, send_signal, 1)
 
-    fslot = jnp.where(upper == 1, (7 - group) * 32 + 63 - place, group * 32 + place)
-
-    def send_filter(i):
-        t = lax.rem(chip + i, 128)
+    zlo, low = chip // 32, lax.rem(chip, 32)
+    fslot = (2 * group + upper) * 32 + jnp.where(upper == 1, 63 - place, place)
+
+    def send_filter(j, r):
+        t = lax.rem(zlo + j, 4) * 32 + lax.rem(low + r, 32)
         for k in range(2):
-            remote(fs.at[k * 128 + t], hb.at[fslot], 1, t, k).start()
-
-    pltpu.make_async_copy(fs.at[core * 128 + chip], hb.at[fslot], rsem.at[1]).start()
-    remote(fs.at[other * 128 + chip], hb.at[fslot], 1, chip, other).start()
-    loop(128, send_filter, 1)
+            pltpu.make_async_remote_copy(
+                src_ref=fs.at[k * 128 + t], dst_ref=hb.at[fslot], send_sem=ssem.at[1],
+                recv_sem=wave_r.at[j], device_id=device(t, k), device_id_type=pl.DeviceIdType.MESH,
+            ).start()
+
+    loop(64, lambda i: send_filter(1 + 2 * lax.rem(i, 2), i // 2))
+    loop(32, lambda i: send_filter(2, i))
+    pltpu.make_async_copy(fs.at[core * 128 + chip], hb.at[fslot], wave_r.at[0]).start()
+    pltpu.make_async_remote_copy(
+        src_ref=fs.at[other * 128 + chip], dst_ref=hb.at[fslot], send_sem=ssem.at[1],
+        recv_sem=wave_r.at[0], device_id=device(chip, other), device_id_type=pl.DeviceIdType.MESH,
+    ).start()
+    loop(32, lambda i: send_filter(0, i), 1)
 
     mine = xb.at[pl.ds(core * 128, 128)]
     theirs = xb.at[pl.ds(other * 128, 128)]
@@ -301,72 +314,88 @@
             ]
             re, im = dft8([p[0] for p in pairs], [p[1] for p in pairs], -1)
             for e in range(8):
-                a, b = re[e], im[e]
+                a, b, m = re[e], im[e], slot_of(e)
                 if e:
                     a, b = cmul(a, b, t2v[0, e : e + 1, ln], t2v[1, e : e + 1, ln])
-                zh[e, rows, ln], zl[e, rows, ln] = split(a)
-                zh[e, rows, lm], zl[e, rows, lm] = split(b)
+                zh[m, rows, ln], zl[m, rows, ln] = split(a)
+                zh[m, rows, lm], zl[m, rows, lm] = split(b)
 
     loop(9, second)
 
-    def third(mul):
-        def body(j):
-            a = zh[pl.ds(j * 2, 2)].reshape(2 * ROWS, 512)
-            b = zl[pl.ds(j * 2, 2)].reshape(2 * ROWS, 512)
-            g = mul(a, m512v[0]) + mul(a, m512v[1]) + mul(b, m512v[0])
-            gg[pl.ds(j * 2, 2)] = g.reshape(2, ROWS, 512)
-
-        loop(4, body)
-
-    third(dot)
-
-    pltpu.make_async_copy(hb, hb, rsem.at[1]).wait()
-    widen(hb, h32)
-
-    def place_filter(e, shift):
+    def third(mul, j):
+        a = zh[pl.ds(j * 2, 2)].reshape(2 * ROWS, 512)
+        b = zl[pl.ds(j * 2, 2)].reshape(2 * ROWS, 512)
+        g = mul(a, m512v[0]) + mul(a, m512v[1]) + mul(b, m512v[0])
+        gg[pl.ds(j * 2, 2)] = g.reshape(2, ROWS, 512)
+
+    loop(4, lambda j: third(dot, j))
+    keep[...] = gg[7, 96:104, :]
+
+    def place_filter(m, shift):
         for ri in range(2):
-            hf[e, ri, 128:144, :] = jnp.zeros((16, 256), F32)
+            hf[m, ri, 128:144, :] = jnp.zeros((16, 256), F32)
             if shift:
-                hf[e, ri, 96:104, :] = jnp.zeros((8, 256), F32)
+                hf[m, ri, 96:104, :] = jnp.zeros((8, 256), F32)
             for blk in range(4):
                 lo = blk * 32 + (1 if shift and blk == 3 else 0)
                 for qh in range(2):
-                    start = e * 512 + (ri * 8 + blk * 2 + qh)
-                    hf[e, ri, lo : lo + 32, qh * 128 : qh * 128 + 128] = h32[
+                    start = m * 512 + (ri * 8 + blk * 2 + qh)
+                    hf[m, ri, lo : lo + 32, qh * 128 : qh * 128 + 128] = h32[
                         pl.ds(start, 32, stride=16), :
                     ]
 
-    loop(4, lambda e: place_filter(e, False))
-
-    @pl.when(core == 1)
-    def _():
-        loop(8, lambda e: place_filter(e, False), 4)
-
-    @pl.when(core == 0)
-    def _():
-        loop(8, lambda e: place_filter(e, True), 4)
+    def apply_filter(m):
+        def body(r):
+            rows = pl.ds(pl.multiple_of(r * 16, 16), 16)
+            a, b = cmul(
+                gg[m, rows, 0:256], gg[m, rows, 256:512], hf[m, 0, rows, :], hf[m, 1, rows, :]
+            )
+            zh[m, rows, 0:256], zl[m, rows, 0:256] = split(a)
+            zh[m, rows, 256:512], zl[m, rows, 256:512] = split(b)
+
+        loop(9, body)
+
+    def mirrors():
         lane = (lax.broadcasted_iota(jnp.int32, (1, 128), 1) == 0).astype(F32)
         re, im = hf[0, 0, 96:97, 0:128], hf[0, 1, 96:97, 0:128]
-        for ri in range(2):
-            hf[4, ri, 96:97, 0:128] = hf[0, ri, 96:97, 128:256]
+        hr = hf[0, 0, 96:104, 128:256] * top[:, 0:128]
+        hi = hf[0, 1, 96:104, 128:256] * top[:, 0:128]
         hf[0, 0, 96:97, 0:128] = re * (1.0 - 0.5 * lane)
         hf[0, 1, 96:97, 0:128] = im * (1.0 - lane)
         hf[0, 0, 96:97, 128:256] = im * (0.5 * lane)
         hf[0, 1, 96:97, 128:256] = jnp.zeros((1, 128), F32)
-
-    def apply_filter(e):
-        def body(r):
-            rows = pl.ds(pl.multiple_of(r * 16, 16), 16)
-            a, b = cmul(
-                gg[e, rows, 0:256], gg[e, rows, 256:512], hf[e, 0, rows, :], hf[e, 1, rows, :]
+        a, b = cmul(keep[:, 0:128], keep[:, 256:384], hr, hi)
+        none = jnp.zeros((8, 128), F32)
+        row = jnp.concatenate([a, none, b, none], 1)
+        high, rest = split(jnp.concatenate([row, jnp.zeros((8, 512), F32)], 0))
+        g = dot_t(high, m512v[0]) + dot_t(high, m512v[1]) + dot_t(rest, m512v[0])
+        keep[...] = g[0:8]
+
+    def wave(w):
+        j = lax.rem(w * 2 + 1, 4) + jnp.where(w == 2, 1, 0) - jnp.where(w == 3, 3, 0)
+        z = lax.rem(zlo + 4 - j, 4)
+        part = hb.at[pl.ds(z * 64, 64)]
+        pltpu.make_async_copy(part, part, wave_r.at[j]).wait()
+
+        def widen_part(i):
+            h32[pl.ds(pl.multiple_of(z * 1024 + i * 256, 256), 256), :] = (
+                hb[pl.ds(z * 64 + i * 16, 16)].astype(F32).reshape(256, 128)
             )
-            zh[e, rows, 0:256], zl[e, rows, 0:256] = split(a)
-            zh[e, rows, 256:512], zl[e, rows, 256:512] = split(b)
-
-        loop(9, body)
-
-    loop(8, apply_filter)
-    third(dot_t)
+
+        loop(4, widen_part)
+        place_filter(2 * z, False)
+        pl.when(core == 1)(lambda: place_filter(2 * z + 1, False))
+        pl.when(core == 0)(lambda: place_filter(2 * z + 1, True))
+        pl.when((core == 0) & (z == 0))(mirrors)
+        apply_filter(2 * z)
+        apply_filter(2 * z + 1)
+        third(dot_t, z)
+
+    loop(4, wave)
+
+    @pl.when(core == 0)
+    def _():
+        gg[7, 96:104, :] = gg[7, 96:104, :] + keep[...]
 
     def back(r, last):
         rows = pl.ds(r * 16, 16) if last else pl.ds(pl.multiple_of(r * 16, 16), 16)
@@ -375,7 +404,7 @@
             lm = slice(256 + half * 128, 384 + half * 128)
             re, im = [], []
             for e in range(8):
-                a, b = gg[e, rows, ln], gg[e, rows, lm]
+                a, b = gg[slot_of(e), rows, ln], gg[slot_of(e), rows, lm]
                 if e:
                     a, b = cmul(a, b, t2v[0, e : e + 1, ln], -t2v[1, e : e + 1, ln])
                 re.append(a)
@@ -514,6 +543,7 @@
             pltpu.VMEM((8, ROWS, 512), BF16),
             pltpu.VMEM((8, ROWS, 512), BF16),
             pltpu.VMEM((8, ROWS, 512), F32),
+            pltpu.VMEM((8, 512), F32),
             pltpu.VMEM((8, 8, 256), F32),
             pltpu.VMEM((8, 256, 256), BF16),
             pltpu.VMEM((8, 256, 256), BF16),
@@ -531,6 +561,7 @@
             pltpu.SemaphoreType.DMA((7,)),
             pltpu.SemaphoreType.DMA((8,)),
             pltpu.SemaphoreType.DMA((8,)),
+            pltpu.SemaphoreType.DMA((4,)),
         ],
         compiler_params=pltpu.CompilerParams(
             collective_id=0, has_side_effects=True, vmem_limit_bytes=56 << 20

time: 91.8 us -> 89.2 us (0.972)
  Pallas kernels: 88.6 us -> 86.8 us
    pallas_call x1, Pallas kernels: 88.6 us -> 86.8 us  [body(): pl.pallas_call(kernel, out_shape=jax.ShapeDtypeStruct(signal.shape, BF16)...]
where the time goes in v5:
time: 89.2 us; the launch traced here: 88.7 us
  Pallas kernels  86.8 us (97%)
  local copies, waits for them, and re-layouts  1.87 us (2%)
    pallas_call x1, Pallas kernels, body(): pl.pallas_call(kernel, out_shape=jax.ShapeDtypeStruct(signal.shape, BF16)...  86.8 us
    unnamed x1, local copies, waits for them, and re-layouts  1.87 us

profile of v5, /device:TPU:32, one launch (start us, length us, event | category | flops | bytes accessed | tf_op | source)
XLA Modules:
  0.0 88.7 jit_solution(10144539258862188926)
XLA Ops:
  0.0 86.8 %shard_map.91 = bf16[2048,128]{1,0:T(8,128)(2,1)} custom-call(bf16[2048,128]{1,0:T(8,128)(2,1)} %sig.1, bf16[2,16,256,128]{3,2,1,0:T(8,128)(2,1)} %filt.1, bf16[2048,128]{1,0:T(8,128)(2,1)} %gate.1, f32[128]{0:T(128)} %skip.1, bf16[2,4,256,256]{3,2,1,0:T(8,128)(2,1)} %constant.10.clone.m256, bf16[2,512,512]{2,1,0:T(8,128)(2,1)} %constant.11.clone.m512, ...), custom_call_target="tpu_custom_call" | custom-call | tf_op jit(solution)/shard_map/pallas_call | solution.py:520
  86.8 1.9 %copy.11 = bf16[2048,128]{1,0:T(8,128)(2,1)} copy(bf16[2048,128]{1,0:T(8,128)(2,1)} %shard_map.91) | data formatting | bytes 1048576

commit v6 on v5

--- a/solution.py
+++ b/solution.py
@@ -129,9 +129,9 @@
 
 def kernel(
     sig, filt, gate, skip, m256, m512, tb, ta, t2, out,
-    fv, ev, gv, m256v, m512v, tbv, tav, t2v,
+    sv, fv, ev, gv, ob, m256v, m512v, tbv, tav, t2v,
     s32, xs, xb, x32, fs, hb, hf, fz, tw, zh, zl, gg, keep, ce, ch, cl,
-    yo, yw, pb, v32, h32, ye, yb, se, sb, lsem, ssem, rsem, swap_s, swap_r, wave_r,
+    yo, yw, pb, v32, h32, ye, yb, se, sb, lsem, ssem, rsem, swap_s, swap_r, wave_r, out_r,
 ):
     ctx, cp = lax.axis_index("ctx"), lax.axis_index("cp")
     core = lax.rem(ctx, 2)
@@ -164,6 +164,8 @@
             barrier, inc=1, device_id=(t // 8, lax.rem(t, 8)), device_id_type=pl.DeviceIdType.MESH
         )
 
+    load_signal = pltpu.make_async_copy(sig, sv, lsem.at[8])
+    load_signal.start()
     loop(256, greet, 1)
 
     group, place = here // 64, lax.rem(here, 64)
@@ -182,9 +184,10 @@
         load.start()
 
     def turn_signal(a):
-        block = sig[pl.ds(pl.multiple_of(a * 128, 128), 128), :].astype(F32)
+        block = sv[pl.ds(pl.multiple_of(a * 128, 128), 128), :].astype(F32)
         s32[pl.ds(a, 128, stride=16), :] = block.T
 
+    load_signal.wait()
     loop(16, turn_signal)
 
     def pack(dst, base):
@@ -355,6 +358,9 @@
 
         loop(9, body)
 
+    def wave_of(w):
+        return lax.rem(w * 2 + 1, 4) + jnp.where(w == 2, 1, 0) - jnp.where(w == 3, 3, 0)
+
     def mirrors():
         lane = (lax.broadcasted_iota(jnp.int32, (1, 128), 1) == 0).astype(F32)
         re, im = hf[0, 0, 96:97, 0:128], hf[0, 1, 96:97, 0:128]
@@ -372,7 +378,7 @@
         keep[...] = g[0:8]
 
     def wave(w):
-        j = lax.rem(w * 2 + 1, 4) + jnp.where(w == 2, 1, 0) - jnp.where(w == 3, 3, 0)
+        j = wave_of(w)
         z = lax.rem(zlo + 4 - j, 4)
         part = hb.at[pl.ds(z * 64, 64)]
         pltpu.make_async_copy(part, part, wave_r.at[j]).wait()
@@ -470,36 +476,65 @@
 
     loop(16, encode)
 
-    def send_out(i):
-        t = lax.rem(chip + i, 128)
-        remote(ye.at[t], yb.at[chip], 5, t, core).start()
+    row = (chip // 8) * 8
 
     def send_scale(i):
-        t = lax.rem(chip + i, 128)
+        t = row + lax.rem(cp + i, 8)
         remote(se.at[0], sb.at[chip], 6, t, core).start()
 
-    pltpu.make_async_copy(ye.at[chip], yb.at[chip], rsem.at[5]).start()
     pltpu.make_async_copy(se.at[0], sb.at[chip], rsem.at[6]).start()
-    loop(128, send_out, 1)
-    loop(128, send_scale, 1)
-    pltpu.make_async_copy(sb, sb, rsem.at[6]).wait()
-    pltpu.make_async_copy(yb, yb, rsem.at[5]).wait()
-
-    def decode(i):
-        for j in range(8):
-            code = yb[i * 8 + j].astype(F32)
-            size = jnp.maximum(jnp.abs(code), 2.0**-126)
-            size = lax.rsqrt(lax.rsqrt(lax.rsqrt(lax.rsqrt(size)))) * sb[i * 8 + j]
-            rows = pl.ds(pl.multiple_of(i * 128 + j * 16, 16), 16)
-            s32[rows, :] = jnp.where(code < 0, -size, size)
+    loop(8, send_scale, 1)
+
+    def send_out(j, r):
+        t = lax.rem(zlo + j, 4) * 32 + lax.rem(low + r, 32)
+        pltpu.make_async_remote_copy(
+            src_ref=ye.at[t], dst_ref=yb.at[chip], send_sem=ssem.at[5],
+            recv_sem=out_r.at[j], device_id=device(t, core), device_id_type=pl.DeviceIdType.MESH,
+        ).start()
+
+    loop(64, lambda i: send_out(1 + 2 * lax.rem(i, 2), i // 2))
+
+    mates = sb.at[pl.ds(row, 8)]
+    pltpu.make_async_copy(mates, mates, rsem.at[6]).wait()
+
+    def pass_scale(i):
+        t = lax.rem(chip + i * 8, 128)
+        remote(mates, mates, 7, t, core).start()
+
+    loop(16, pass_scale, 1)
+
+    loop(32, lambda i: send_out(2, i))
+    pltpu.make_async_copy(ye.at[chip], yb.at[chip], out_r.at[0]).start()
+    loop(32, lambda i: send_out(0, i), 1)
+
+    most = sb.at[pl.ds(0, 120)]
+    pltpu.make_async_copy(most, most, rsem.at[7]).wait()
+
+    def decode(w):
+        j = wave_of(w)
+        base = lax.rem(zlo + 4 - j, 4) * 32
+        part = yb.at[pl.ds(base, 32)]
+        pltpu.make_async_copy(part, part, out_r.at[j]).wait()
+
+        def eight(i):
+            for n in range(8):
+                c = base + i * 8 + n
+                code = yb[c].astype(F32)
+                size = jnp.maximum(jnp.abs(code), 2.0**-126)
+                size = lax.rsqrt(lax.rsqrt(lax.rsqrt(lax.rsqrt(size)))) * sb[c]
+                s32[pl.ds(pl.multiple_of(c * 16, 16), 16), :] = jnp.where(code < 0, -size, size)
+
+        loop(4, eight)
 
     def finish(a):
         rows = pl.ds(pl.multiple_of(a * 128, 128), 128)
         value = s32[pl.ds(a, 128, stride=16), :].T
-        out[rows, :] = (gv[rows, :].astype(F32) * value).astype(BF16)
-
-    loop(16, decode)
+        ob[rows, :] = (gv[rows, :].astype(F32) * value).astype(BF16)
+        pltpu.make_async_copy(ob.at[rows], out.at[rows], lsem.at[9]).start()
+
+    loop(4, decode)
     loop(16, finish)
+    pltpu.make_async_copy(ob, out, lsem.at[9]).wait()
 
     def sent(ref, sem):
         pltpu.make_async_copy(ref, ref, ssem.at[sem]).wait()
@@ -509,22 +544,24 @@
 
     forward.wait_send()
     sent(ye.at[pl.ds(0, 127)], 5)
-    sent(sb.at[pl.ds(0, 127)], 6)
+    sent(sb.at[pl.ds(0, 7)], 6)
+    sent(most, 7)
 
 
 def body(signal, gate, filters, skip):
     m256, m512, tb, ta, t2 = (jnp.asarray(t) for t in tables())
-    vmem = pl.BlockSpec(memory_space=pltpu.VMEM)
     hbm = pl.BlockSpec(memory_space=pl.ANY)
     smem = pl.BlockSpec(memory_space=pltpu.SMEM)
     return pl.pallas_call(
         kernel,
         out_shape=jax.ShapeDtypeStruct(signal.shape, BF16),
-        in_specs=[vmem, hbm, hbm, smem, hbm, hbm, hbm, hbm, hbm],
-        out_specs=vmem,
+        in_specs=[hbm, hbm, hbm, smem, hbm, hbm, hbm, hbm, hbm],
+        out_specs=hbm,
         scratch_shapes=[
+            pltpu.VMEM((2048, 128), BF16),
             pltpu.VMEM((2, 8, 256, 128), BF16),
             pltpu.VMEM((2, 1, 128, 128), BF16),
+            pltpu.VMEM((2048, 128), BF16),
             pltpu.VMEM((2048, 128), BF16),
             pltpu.VMEM((4, 256, 256), BF16),
             pltpu.VMEM((2, 512, 512), BF16),
@@ -556,11 +593,12 @@
             pltpu.VMEM((128, 16, 128), BF16),
             pltpu.VMEM((1, 1, 128), F32),
             pltpu.VMEM((128, 1, 128), F32),
-            pltpu.SemaphoreType.DMA((8,)),
-            pltpu.SemaphoreType.DMA((7,)),
-            pltpu.SemaphoreType.DMA((7,)),
+            pltpu.SemaphoreType.DMA((10,)),
             pltpu.SemaphoreType.DMA((8,)),
             pltpu.SemaphoreType.DMA((8,)),
+            pltpu.SemaphoreType.DMA((8,)),
+            pltpu.SemaphoreType.DMA((8,)),
+            pltpu.SemaphoreType.DMA((4,)),
             pltpu.SemaphoreType.DMA((4,)),
         ],
         compiler_params=pltpu.CompilerParams(

time: 89.2 us -> 86 us (0.964)
  Pallas kernels: 86.8 us -> 83.9 us
    pallas_call x1, Pallas kernels: 86.8 us -> 83.9 us  [body(): pl.pallas_call(kernel, out_shape=jax.ShapeDtypeStruct(signal.shape, BF16)...]
where the time goes in v6:
time: 86 us; the launch traced here: 85.7 us
  Pallas kernels  83.9 us (98%)
  local copies, waits for them, and re-layouts  1.87 us (2%)
    pallas_call x1, Pallas kernels, body(): pl.pallas_call(kernel, out_shape=jax.ShapeDtypeStruct(signal.shape, BF16)...  83.9 us
    unnamed x1, local copies, waits for them, and re-layouts  1.87 us

profile of v6, /device:TPU:32, one launch (start us, length us, event | category | flops | bytes accessed | tf_op | source)
XLA Modules:
  0.0 85.7 jit_solution(5066514065584945933)
XLA Ops:
  0.0 83.9 %shard_map.91 = bf16[2048,128]{1,0:T(8,128)(2,1)} custom-call(bf16[2048,128]{1,0:T(8,128)(2,1)} %sig.1, bf16[2,16,256,128]{3,2,1,0:T(8,128)(2,1)} %filt.1, bf16[2048,128]{1,0:T(8,128)(2,1)} %gate.1, f32[128]{0:T(128)} %skip.1, bf16[2,4,256,256]{3,2,1,0:T(8,128)(2,1)} %constant.10.clone.m256, bf16[2,512,512]{2,1,0:T(8,128)(2,1)} %constant.11.clone.m512, ...), custom_call_target="tpu_custom_call" | custom-call | tf_op jit(solution)/shard_map/pallas_call | solution.py:555
  83.9 1.9 %copy.11 = bf16[2048,128]{1,0:T(8,128)(2,1)} copy(bf16[2048,128]{1,0:T(8,128)(2,1)} %shard_map.91) | data formatting | bytes 1048576

commit v7 on v6

--- a/solution.py
+++ b/solution.py
@@ -143,11 +143,14 @@
     def device(t, k):
         return ((t // 8) * 2 + k, lax.rem(t, 8))
 
+    def push(src, dst, send, recv, line, column):
+        return pltpu.make_async_remote_copy(
+            src_ref=src, dst_ref=dst, send_sem=send, recv_sem=recv,
+            device_id=(line, column), device_id_type=pl.DeviceIdType.MESH,
+        )
+
     def remote(src, dst, sem, t, k):
-        return pltpu.make_async_remote_copy(
-            src_ref=src, dst_ref=dst, send_sem=ssem.at[sem], recv_sem=rsem.at[sem],
-            device_id=device(t, k), device_id_type=pl.DeviceIdType.MESH,
-        )
+        return push(src, dst, ssem.at[sem], rsem.at[sem], *device(t, k))
 
     def loop(n, body, start=0):
         def wrapped(i, carry):
@@ -158,15 +161,19 @@
 
     barrier = pltpu.get_barrier_semaphore()
 
-    def greet(i):
-        t = lax.rem(here + i, 256)
-        pl.semaphore_signal(
-            barrier, inc=1, device_id=(t // 8, lax.rem(t, 8)), device_id_type=pl.DeviceIdType.MESH
-        )
+    columns = [lax.rem(cp + r, 8) for r in range(8)]
+
+    def greet(i, first=0):
+        line = lax.rem(ctx + i, 32)
+        for column in columns[first:]:
+            pl.semaphore_signal(
+                barrier, inc=1, device_id=(line, column), device_id_type=pl.DeviceIdType.MESH
+            )
 
     load_signal = pltpu.make_async_copy(sig, sv, lsem.at[8])
     load_signal.start()
-    loop(256, greet, 1)
+    loop(32, greet, 1)
+    greet(0, 1)
 
     group, place = here // 64, lax.rem(here, 64)
     upper = (place >= 32).astype(jnp.int32)
@@ -243,32 +250,48 @@
     pl.semaphore_wait(barrier, 255)
     slot = core * 128 + chip
 
-    def send_signal(i):
-        t = lax.rem(chip + i, 128)
-        remote(xs.at[t], xb.at[slot], 0, t, core).start()
+    home = ctx // 2
+    zlo, wide = home // 4, lax.rem(home, 4)
+
+    def send_signal(i, first=0):
+        row = lax.rem(home + i, 16)
+        for column in columns[first:]:
+            push(
+                xs.at[row * 8 + column], xb.at[slot], ssem.at[0], rsem.at[0], row * 2 + core, column
+            ).start()
 
     pltpu.make_async_copy(xs.at[chip], xb.at[slot], rsem.at[0]).start()
-    loop(128, send_signal, 1)
-
-    zlo, low = chip // 32, lax.rem(chip, 32)
+    send_signal(0, 1)
+    loop(16, send_signal, 1)
+
+    def in_waves(send, own):
+        loop(8, lambda i: send(1 + 2 * lax.rem(i, 2), i // 2))
+        loop(4, lambda i: send(2, i))
+        own()
+        send(0, 0, 1)
+        loop(4, lambda i: send(0, i), 1)
+
+    def row_of(j, i):
+        return lax.rem(zlo + j, 4) * 4 + lax.rem(wide + i, 4)
+
     fslot = (2 * group + upper) * 32 + jnp.where(upper == 1, 63 - place, place)
 
-    def send_filter(j, r):
-        t = lax.rem(zlo + j, 4) * 32 + lax.rem(low + r, 32)
-        for k in range(2):
-            pltpu.make_async_remote_copy(
-                src_ref=fs.at[k * 128 + t], dst_ref=hb.at[fslot], send_sem=ssem.at[1],
-                recv_sem=wave_r.at[j], device_id=device(t, k), device_id_type=pl.DeviceIdType.MESH,
-            ).start()
-
-    loop(64, lambda i: send_filter(1 + 2 * lax.rem(i, 2), i // 2))
-    loop(32, lambda i: send_filter(2, i))
-    pltpu.make_async_copy(fs.at[core * 128 + chip], hb.at[fslot], wave_r.at[0]).start()
-    pltpu.make_async_remote_copy(
-        src_ref=fs.at[other * 128 + chip], dst_ref=hb.at[fslot], send_sem=ssem.at[1],
-        recv_sem=wave_r.at[0], device_id=device(chip, other), device_id_type=pl.DeviceIdType.MESH,
-    ).start()
-    loop(32, lambda i: send_filter(0, i), 1)
+    def send_filter(j, i, first=0):
+        row = row_of(j, i)
+        for column in columns[first:]:
+            for k in range(2):
+                push(
+                    fs.at[k * 128 + row * 8 + column], hb.at[fslot],
+                    ssem.at[1], wave_r.at[j], row * 2 + k, column,
+                ).start()
+
+    def own_filter():
+        pltpu.make_async_copy(fs.at[core * 128 + chip], hb.at[fslot], wave_r.at[0]).start()
+        push(
+            fs.at[other * 128 + chip], hb.at[fslot], ssem.at[1], wave_r.at[0], home * 2 + other, cp
+        ).start()
+
+    in_waves(send_filter, own_filter)
 
     mine = xb.at[pl.ds(core * 128, 128)]
     theirs = xb.at[pl.ds(other * 128, 128)]
@@ -476,36 +499,30 @@
 
     loop(16, encode)
 
-    row = (chip // 8) * 8
-
-    def send_scale(i):
-        t = row + lax.rem(cp + i, 8)
-        remote(se.at[0], sb.at[chip], 6, t, core).start()
-
     pltpu.make_async_copy(se.at[0], sb.at[chip], rsem.at[6]).start()
-    loop(8, send_scale, 1)
-
-    def send_out(j, r):
-        t = lax.rem(zlo + j, 4) * 32 + lax.rem(low + r, 32)
-        pltpu.make_async_remote_copy(
-            src_ref=ye.at[t], dst_ref=yb.at[chip], send_sem=ssem.at[5],
-            recv_sem=out_r.at[j], device_id=device(t, core), device_id_type=pl.DeviceIdType.MESH,
-        ).start()
-
-    loop(64, lambda i: send_out(1 + 2 * lax.rem(i, 2), i // 2))
-
-    mates = sb.at[pl.ds(row, 8)]
+    for column in columns[1:]:
+        push(se.at[0], sb.at[chip], ssem.at[6], rsem.at[6], ctx, column).start()
+
+    def send_out(j, i, first=0):
+        row = row_of(j, i)
+        for column in columns[first:]:
+            push(
+                ye.at[row * 8 + column], yb.at[chip], ssem.at[5], out_r.at[j], row * 2 + core, column
+            ).start()
+
+    def own_out():
+        pltpu.make_async_copy(ye.at[chip], yb.at[chip], out_r.at[0]).start()
+
+    in_waves(send_out, own_out)
+
+    mates = sb.at[pl.ds(home * 8, 8)]
     pltpu.make_async_copy(mates, mates, rsem.at[6]).wait()
 
     def pass_scale(i):
-        t = lax.rem(chip + i * 8, 128)
-        remote(mates, mates, 7, t, core).start()
+        row = lax.rem(home + i, 16)
+        push(mates, mates, ssem.at[7], rsem.at[7], row * 2 + core, cp).start()
 
     loop(16, pass_scale, 1)
-
-    loop(32, lambda i: send_out(2, i))
-    pltpu.make_async_copy(ye.at[chip], yb.at[chip], out_r.at[0]).start()
-    loop(32, lambda i: send_out(0, i), 1)
 
     most = sb.at[pl.ds(0, 120)]
     pltpu.make_async_copy(most, most, rsem.at[7]).wait()

time: 86 us -> 82.3 us (0.957)
  Pallas kernels: 83.9 us -> 79.7 us
    pallas_call x1, Pallas kernels: 83.9 us -> 79.7 us  [body(): pl.pallas_call(kernel, out_shape=jax.ShapeDtypeStruct(signal.shape, BF16)...]
where the time goes in v7:
time: 82.3 us; the launch traced here: 81.6 us
  Pallas kernels  79.7 us (97%)
  local copies, waits for them, and re-layouts  1.87 us (2%)
    pallas_call x1, Pallas kernels, body(): pl.pallas_call(kernel, out_shape=jax.ShapeDtypeStruct(signal.shape, BF16)...  79.7 us
    unnamed x1, local copies, waits for them, and re-layouts  1.87 us

profile of v7, /device:TPU:32, one launch (start us, length us, event | category | flops | bytes accessed | tf_op | source)
XLA Modules:
  0.0 81.6 jit_solution(2265051952465442948)
XLA Ops:
  0.0 79.7 %shard_map.91 = bf16[2048,128]{1,0:T(8,128)(2,1)} custom-call(bf16[2048,128]{1,0:T(8,128)(2,1)} %sig.1, bf16[2,16,256,128]{3,2,1,0:T(8,128)(2,1)} %filt.1, bf16[2048,128]{1,0:T(8,128)(2,1)} %gate.1, f32[128]{0:T(128)} %skip.1, bf16[2,4,256,256]{3,2,1,0:T(8,128)(2,1)} %constant.10.clone.m256, bf16[2,512,512]{2,1,0:T(8,128)(2,1)} %constant.11.clone.m512, ...), custom_call_target="tpu_custom_call" | custom-call | tf_op jit(solution)/shard_map/pallas_call | solution.py:572
  79.7 1.9 %copy.11 = bf16[2048,128]{1,0:T(8,128)(2,1)} copy(bf16[2048,128]{1,0:T(8,128)(2,1)} %shard_map.91) | data formatting | bytes 1048576

commit v8 on v7

--- a/solution.py
+++ b/solution.py
@@ -206,6 +206,33 @@
 
     pack(xs, 0)
 
+    pl.semaphore_wait(barrier, 255)
+    slot = core * 128 + chip
+
+    home = ctx // 2
+    zlo, wide = home // 4, lax.rem(home, 4)
+
+    def send_signal(i, first=0):
+        row = lax.rem(home + i, 16)
+        for column in columns[first:]:
+            push(
+                xs.at[row * 8 + column], xb.at[slot], ssem.at[0], rsem.at[0], row * 2 + core, column
+            ).start()
+
+    pltpu.make_async_copy(xs.at[chip], xb.at[slot], rsem.at[0]).start()
+    send_signal(0, 1)
+    loop(16, send_signal, 1)
+
+    def in_waves(send, own):
+        loop(8, lambda i: send(1 + 2 * lax.rem(i, 2), i // 2))
+        own()
+        send(0, 0, 1)
+        loop(4, lambda i: send(0, i), 1)
+        loop(4, lambda i: send(2, i))
+
+    def row_of(j, i):
+        return lax.rem(zlo + j, 4) * 4 + lax.rem(wide + i, 4)
+
     loads[0].wait()
     loads[1].wait()
 
@@ -233,46 +260,6 @@
     pack(fs, 0)
     turn_filter(1)
     pack(fs, 128)
-
-    loads[2].wait()
-    loads[3].wait()
-
-    def make_twiddle(r):
-        rows = pl.ds(pl.multiple_of(r * 16, 16), 16)
-        cols = tav[rows, :]
-        for al in range(8):
-            c = jnp.broadcast_to(cols[:, al : al + 1], (16, 256))
-            s = jnp.broadcast_to(cols[:, 8 + al : 9 + al], (16, 256))
-            tw[al, 0, rows, :], tw[al, 1, rows, :] = cmul(c, s, tbv[0, rows, :], tbv[1, rows, :])
-
-    loop(9, make_twiddle)
-
-    pl.semaphore_wait(barrier, 255)
-    slot = core * 128 + chip
-
-    home = ctx // 2
-    zlo, wide = home // 4, lax.rem(home, 4)
-
-    def send_signal(i, first=0):
-        row = lax.rem(home + i, 16)
-        for column in columns[first:]:
-            push(
-                xs.at[row * 8 + column], xb.at[slot], ssem.at[0], rsem.at[0], row * 2 + core, column
-            ).start()
-
-    pltpu.make_async_copy(xs.at[chip], xb.at[slot], rsem.at[0]).start()
-    send_signal(0, 1)
-    loop(16, send_signal, 1)
-
-    def in_waves(send, own):
-        loop(8, lambda i: send(1 + 2 * lax.rem(i, 2), i // 2))
-        loop(4, lambda i: send(2, i))
-        own()
-        send(0, 0, 1)
-        loop(4, lambda i: send(0, i), 1)
-
-    def row_of(j, i):
-        return lax.rem(zlo + j, 4) * 4 + lax.rem(wide + i, 4)
 
     fslot = (2 * group + upper) * 32 + jnp.where(upper == 1, 63 - place, place)
 
@@ -292,6 +279,19 @@
         ).start()
 
     in_waves(send_filter, own_filter)
+
+    loads[2].wait()
+    loads[3].wait()
+
+    def make_twiddle(r):
+        rows = pl.ds(pl.multiple_of(r * 16, 16), 16)
+        cols = tav[rows, :]
+        for al in range(8):
+            c = jnp.broadcast_to(cols[:, al : al + 1], (16, 256))
+            s = jnp.broadcast_to(cols[:, 8 + al : 9 + al], (16, 256))
+            tw[al, 0, rows, :], tw[al, 1, rows, :] = cmul(c, s, tbv[0, rows, :], tbv[1, rows, :])
+
+    loop(9, make_twiddle)
 
     mine = xb.at[pl.ds(core * 128, 128)]
     theirs = xb.at[pl.ds(other * 128, 128)]
@@ -382,7 +382,7 @@
         loop(9, body)
 
     def wave_of(w):
-        return lax.rem(w * 2 + 1, 4) + jnp.where(w == 2, 1, 0) - jnp.where(w == 3, 3, 0)
+        return lax.rem(w * 2 + 1, 4) - jnp.where(w >= 2, 1, 0)
 
     def mirrors():
         lane = (lax.broadcasted_iota(jnp.int32, (1, 128), 1) == 0).astype(F32)
@@ -497,7 +497,6 @@
         code = jnp.where(value < 0, -power, power)
         ye[pl.ds(i * 8, 8)] = code.astype(BF16).reshape(8, 16, 128)
 
-    loop(16, encode)
 
     pltpu.make_async_copy(se.at[0], sb.at[chip], rsem.at[6]).start()
     for column in columns[1:]:
@@ -505,12 +504,15 @@
 
     def send_out(j, i, first=0):
         row = row_of(j, i)
+        if not first:
+            encode(row)
         for column in columns[first:]:
             push(
                 ye.at[row * 8 + column], yb.at[chip], ssem.at[5], out_r.at[j], row * 2 + core, column
             ).start()
 
     def own_out():
+        encode(home)
         pltpu.make_async_copy(ye.at[chip], yb.at[chip], out_r.at[0]).start()
 
     in_waves(send_out, own_out)

time: 82.3 us -> 79.8 us (0.970)
  Pallas kernels: 79.7 us -> 77.8 us
    pallas_call x1, Pallas kernels: 79.7 us -> 77.8 us  [body(): pl.pallas_call(kernel, out_shape=jax.ShapeDtypeStruct(signal.shape, BF16)...]
where the time goes in v8:
time: 79.8 us; the launch traced here: 79.7 us
  Pallas kernels  77.8 us (97%)
  local copies, waits for them, and re-layouts  1.87 us (2%)
    pallas_call x1, Pallas kernels, body(): pl.pallas_call(kernel, out_shape=jax.ShapeDtypeStruct(signal.shape, BF16)...  77.8 us
    unnamed x1, local copies, waits for them, and re-layouts  1.87 us

profile of v8, /device:TPU:32, one launch (start us, length us, event | category | flops | bytes accessed | tf_op | source)
XLA Modules:
  0.0 79.7 jit_solution(17735986657854639213)
XLA Ops:
  0.0 77.8 %shard_map.91 = bf16[2048,128]{1,0:T(8,128)(2,1)} custom-call(bf16[2048,128]{1,0:T(8,128)(2,1)} %sig.1, bf16[2,16,256,128]{3,2,1,0:T(8,128)(2,1)} %filt.1, bf16[2048,128]{1,0:T(8,128)(2,1)} %gate.1, f32[128]{0:T(128)} %skip.1, bf16[2,4,256,256]{3,2,1,0:T(8,128)(2,1)} %constant.10.clone.m256, bf16[2,512,512]{2,1,0:T(8,128)(2,1)} %constant.11.clone.m512, ...), custom_call_target="tpu_custom_call" | custom-call | tf_op jit(solution)/shard_map/pallas_call | solution.py:574
  77.8 1.9 %copy.11 = bf16[2048,128]{1,0:T(8,128)(2,1)} copy(bf16[2048,128]{1,0:T(8,128)(2,1)} %shard_map.91) | data formatting | bytes 1048576

commit v9 on v8

--- a/solution.py
+++ b/solution.py
@@ -163,17 +163,26 @@
 
     columns = [lax.rem(cp + r, 8) for r in range(8)]
 
-    def greet(i, first=0):
+    near = (cp // 4) * 4
+    sides = [[base + lax.rem(cp + r, 4) for r in range(4)] for base in (4 - near, near)]
+
+    def greet(i, side, first=0):
         line = lax.rem(ctx + i, 32)
-        for column in columns[first:]:
+        for column in sides[side][first:]:
             pl.semaphore_signal(
                 barrier, inc=1, device_id=(line, column), device_id_type=pl.DeviceIdType.MESH
             )
 
+    def greet_two(i, side):
+        greet(2 * i, side)
+        greet(2 * i + 1, side)
+
     load_signal = pltpu.make_async_copy(sig, sv, lsem.at[8])
     load_signal.start()
-    loop(32, greet, 1)
-    greet(0, 1)
+    loop(16, lambda i: greet_two(i, 0))
+    loop(16, lambda i: greet_two(i, 1), 1)
+    greet(1, 1)
+    greet(0, 1, 1)
 
     group, place = here // 64, lax.rem(here, 64)
     upper = (place >= 32).astype(jnp.int32)

time: 79.8 us -> 79.6 us (level); the launches traced: 79.7 us -> 78.5 us
  Pallas kernels: 77.8 us -> 76.6 us
    pallas_call x1, Pallas kernels: 77.8 us -> 76.6 us  [body(): pl.pallas_call(kernel, out_shape=jax.ShapeDtypeStruct(signal.shape, BF16)...]
where the time goes in v9:
time: 79.6 us; the launch traced here: 78.5 us
  Pallas kernels  76.6 us (96%)
  local copies, waits for them, and re-layouts  1.87 us (2%)
    pallas_call x1, Pallas kernels, body(): pl.pallas_call(kernel, out_shape=jax.ShapeDtypeStruct(signal.shape, BF16)...  76.6 us
    unnamed x1, local copies, waits for them, and re-layouts  1.87 us

profile of v9, /device:TPU:32, one launch (start us, length us, event | category | flops | bytes accessed | tf_op | source)
XLA Modules:
  0.0 78.5 jit_solution(2459845624397346633)
XLA Ops:
  0.0 76.6 %shard_map.91 = bf16[2048,128]{1,0:T(8,128)(2,1)} custom-call(bf16[2048,128]{1,0:T(8,128)(2,1)} %sig.1, bf16[2,16,256,128]{3,2,1,0:T(8,128)(2,1)} %filt.1, bf16[2048,128]{1,0:T(8,128)(2,1)} %gate.1, f32[128]{0:T(128)} %skip.1, bf16[2,4,256,256]{3,2,1,0:T(8,128)(2,1)} %constant.10.clone.m256, bf16[2,512,512]{2,1,0:T(8,128)(2,1)} %constant.11.clone.m512, ...), custom_call_target="tpu_custom_call" | custom-call | tf_op jit(solution)/shard_map/pallas_call | solution.py:583
  76.6 1.9 %copy.11 = bf16[2048,128]{1,0:T(8,128)(2,1)} copy(bf16[2048,128]{1,0:T(8,128)(2,1)} %shard_map.91) | data formatting | bytes 1048576
